TPU v7x, 32 devices: a whole 2x2x4 slice. The times are simulated.
32 devices in a mesh: row: 8 (over z, y), col: 4 (over x, core).
Axes of the slice: x: 2, y: 2, z: 4, core: 2. Of those that a mesh axis runs over, the one named last changes fastest.
Arguments:
- factor: float32 [2, 1024, 1024], P(None, 'row', 'col'), may hold values from -0.125 to 0.125
- lower_inverse: float32 [2, 512, 1024], P(None, None, 'row'), may hold values from -1 to 2
- upper_inverse: float32 [2, 512, 1024], P(None, None, 'row'), may hold values from -1 to 2
- krylov_block: float32 [2, 16, 1024], P(None, None, 'row'), may hold values from -6 to 6
- basis: float32 [2, 64, 1024], P(None, None, 'row'), may hold values from -0.125 to 0.125
Outputs:
- projected: float32 [2, 16, 1024], P(None, None, 'row')
- coefficients: float32 [2, 64, 16], replicated
All inputs are finite; a program needn't handle non-finite values.
Results may differ from a plain program's by a relative error of at most 0.00012.
Values sent between devices are 32-bit elements; how exact they have to be, the bound alone decides.
A program may use at most 64 MiB of HBM per device.

v0:
```python
import functools

import jax
import jax.numpy as jnp
from jax import lax
from jax.experimental import pallas as pl
from jax.experimental.pallas import tpu as pltpu
from jax.sharding import PartitionSpec as P

MESH = pl.DeviceIdType.MESH
F32 = jnp.float32
BF16 = jnp.bfloat16


def split(value):
    high = value.astype(BF16)
    low = (value - high.astype(F32)).astype(BF16)
    return high, low


def dot_nt(left, right):
    return lax.dot_general(left, right, (((1,), (1,)), ((), ())), preferred_element_type=F32)


def dot_nn(left, right):
    return lax.dot_general(left, right, (((1,), (0,)), ((), ())), preferred_element_type=F32)


def product(left, high, low, dot):
    rows = left.shape[0]
    left_high, left_low = split(left)
    both = dot(jnp.concatenate([left_high, left_low], 0), high)
    return both[:rows] + (both[rows:] + dot(left_high, low))


def complex_left(pieces, nvec):
    re = [x[:nvec] for x in pieces]
    im = [x[nvec:] for x in pieces]
    top = jnp.concatenate(re + [-x for x in im], 1)
    bottom = jnp.concatenate(im + re, 1)
    return jnp.concatenate([top, bottom], 0)


def kernel(
    R, C, factor, lower, upper, krylov, basis, projected, coefficients,
    inv_hi, inv_lo, fac_hi, fac_lo, bas_hi, bas_lo,
    end_hi, end_lo, lead_hi, lead_lo, gather,
    psend, precv, ybuf, xbuf, bcast, vbuf, vrecv, fsend, frecv, gacc, grecv,
    psend_sem, precv_sem, bsend_sem, brecv_sem, vsend_sem, vrecv_sem, xsend_sem, xrecv_sem,
    fsend_sem, frecv_sem, gsend_sem, grecv_sem, tsend_sem, trecv_sem, ysend_sem, yrecv_sem,
    ready_sem,
):
    tile, rows = lower.shape[1], lower.shape[2]
    width = factor.shape[2]
    nvec = krylov.shape[1]
    nb = basis.shape[1]
    share = tile // rows
    per = tile // width
    pieces = width // rows
    steps = R.bit_length() - 1
    r = lax.axis_index("row")
    c = lax.axis_index("col")
    t, p = r // share, r % share
    j, h = c // per, c % per
    solver = j == t

    barrier = pltpu.get_barrier_semaphore()

    def greet_mate(i, carry):
        pl.semaphore_signal(barrier, inc=1, device_id=(t * share + (p + 1 + i) % share, c), device_id_type=MESH)
        return carry

    def greet_tile(i, carry):
        pl.semaphore_signal(barrier, inc=1, device_id=((r + (1 + i) * share) % R, c), device_id_type=MESH)
        return carry

    def greet_col(i, carry):
        pl.semaphore_signal(barrier, inc=1, device_id=(r, (c + 1 + i) % C), device_id_type=MESH)
        return carry

    lax.fori_loop(0, share - 1, greet_mate, 0)
    lax.fori_loop(0, R // share - 1, greet_tile, 0)
    lax.fori_loop(0, C - 1, greet_col, 0)

    def prepare(ref, slot):
        high, low = split(jnp.concatenate([ref[0], ref[1]], 1))
        inv_hi[slot] = high
        inv_lo[slot] = low

    @pl.when(solver)
    def _():
        prepare(lower, 0)

    @pl.when(jnp.logical_not(solver))
    def _():
        high, low = split(jnp.concatenate([factor[0], factor[1]], 1))
        fac_hi[...] = high
        fac_lo[...] = low

    def prepare_basis():
        top = jnp.concatenate([basis[0], basis[1]], 1)
        bottom = jnp.concatenate([-basis[1], basis[0]], 1)
        high, low = split(jnp.concatenate([top, bottom], 0))
        bas_hi[...] = high
        bas_lo[...] = low
        gacc[0] = product(top, high, low, dot_nt)

    def remote(src, dst, send, recv, dest):
        return pltpu.make_async_remote_copy(
            src_ref=src, dst_ref=dst, send_sem=send, recv_sem=recv, device_id=dest, device_id_type=MESH
        )

    def each(first_index, last_index, act):
        def body(i, carry):
            act(i)
            return carry

        lax.fori_loop(first_index, last_index, body, 0)

    def gram_copy(i):
        other = r + (1 << i) * (1 - 2 * ((r // (1 << i)) % 2))
        return remote(gacc.at[i], grecv.at[i], gsend_sem.at[i], grecv_sem.at[i], (other, c))

    def gram_all():
        for i in range(steps):
            copy = gram_copy(i)
            copy.start()
            copy.wait_recv()
            gacc[i + 1] = gacc[i] + grecv[i]
        top = gacc[steps]
        gram = jnp.concatenate([top, jnp.concatenate([-top[:, nb:], top[:, :nb]], 1)], 0)
        row_id = lax.broadcasted_iota(jnp.int32, gram.shape, 0)
        col_id = lax.broadcasted_iota(jnp.int32, gram.shape, 1)
        twice = jnp.where(row_id == col_id, 2.0, 0.0) - gram
        spread = product(twice, bas_hi[...], bas_lo[...], dot_nn)
        high, low = split(jnp.concatenate([twice, spread], 1))
        end_hi[...] = high
        end_lo[...] = low

    def t_copy(d):
        q = (p + d) % share
        return remote(basis, gather.at[p], tsend_sem.at[d], trecv_sem.at[p], (t * share + q, c))

    def lead_send():
        for d in range(1, share):
            t_copy(d).start()
        gather[p] = basis[...]

    def lead_all():
        for d in range(1, share):
            q = (p + d) % share
            remote(basis, gather.at[q], tsend_sem.at[d], trecv_sem.at[q], (t * share + q, c)).wait_recv()
        left = jnp.concatenate(
            [jnp.concatenate([gather[q, i] for q in range(share)], 1) for i in range(2)], 0
        )
        out = product(left, inv_hi[1], inv_lo[1], dot_nn)
        one = out[:nb, :rows] + out[nb:, rows:]
        two = out[nb:, :rows] - out[:nb, rows:]
        whole = jnp.concatenate([jnp.concatenate([one, two], 1), jnp.concatenate([-two, one], 1)], 0)
        high, low = split(whole)
        lead_hi[...] = high
        lead_lo[...] = low

    def side_work():
        gram_all()

        @pl.when(t == 0)
        def _():
            lead_send()
            lead_all()

    def part_copy(sweep, d):
        q = (p + d) % share
        return remote(
            psend.at[sweep, q], precv.at[sweep, p], psend_sem.at[sweep, q], precv_sem.at[sweep, p], (t * share + q, c)
        )

    def part_arrival(sweep, d):
        q = (p + d) % share
        return remote(
            psend.at[sweep, q], precv.at[sweep, q], psend_sem.at[sweep, q], precv_sem.at[sweep, q], (t * share + q, c)
        ), q

    def v_copy(cc):
        return remote(vbuf, vrecv.at[c], vsend_sem.at[cc], vrecv_sem.at[c], (r, cc))

    def v_each(act):
        @pl.when(t > 0)
        def _():
            for hh in range(per):
                act(v_copy(t * per + hh))

        @pl.when(t == 0)
        def _():
            each(1, C, lambda d: act(v_copy((c + d) % C)))

    def v_sum(first_col, last_col, value):
        def body(cc, total):
            @pl.when(cc != c)
            def _():
                remote(vbuf, vrecv.at[cc], vsend_sem.at[0], vrecv_sem.at[cc], (r, cc)).wait_recv()

            return total - vrecv[cc]

        return lax.fori_loop(first_col, last_col, body, value)

    def f_copy(d):
        return remote(fsend, frecv.at[r], fsend_sem.at[d], frecv_sem.at[r], ((r + d) % R, c))

    def send_first(value, high, low):
        wide_value = jnp.concatenate([value[:nvec], value[nvec:]], 1)
        fsend[...] = product(wide_value, high, low, dot_nt)
        each(1, R, lambda d: f_copy(d).start())

    def multiply(sweep, g):
        out = product(complex_left([g], nvec), inv_hi[sweep], inv_lo[sweep], dot_nt)
        for q in range(share):
            psend[sweep, q] = out[:, q * rows:(q + 1) * rows]

    def solve(sweep, g):
        multiply(sweep, g)
        return exchange(sweep)

    def exchange(sweep):
        for d in range(1, share):
            part_copy(sweep, d).start()
        total = psend[sweep, p]
        for d in range(1, share):
            arrival, q = part_arrival(sweep, d)
            arrival.wait_recv()
            total = total + precv[sweep, q]
        return total

    def b_copy(buf, rr):
        return remote(buf, bcast.at[p % pieces], bsend_sem.at[rr], brecv_sem.at[p % pieces], (rr, c))

    def x_copy(tt):
        cc = tt * per + h
        return remote(xbuf, xbuf, xsend_sem.at[tt], xrecv_sem.at[0], (r, cc))

    def y_copy(tt):
        return remote(ybuf, ybuf, ysend_sem.at[tt], yrecv_sem.at[0], (r, tt * per + h))

    speaks = p // pieces == h

    @pl.when(solver != (t == 0))
    def _():
        prepare(upper, 1)

    @pl.when(j > 0)
    def _():
        prepare_basis()

    @pl.when(jnp.logical_and(solver, t == 0))
    def _():
        multiply(0, jnp.concatenate([krylov[0], krylov[1]], 0))

    pl.semaphore_wait(barrier, share - 1 + R // share - 1 + C - 1)
    for d in range(1, share):
        pl.semaphore_signal(
            ready_sem, inc=1, device_id=(t * share + (p + d) % share, c), device_id_type=MESH
        )

    @pl.when(j > 0)
    def _():
        side_work()

    @pl.when(solver)
    def _():
        @pl.when(t > 0)
        def _():
            b = jnp.concatenate([krylov[0], krylov[1]], 0)
            multiply(0, v_sum(0, t * per, b))

        ybuf[...] = exchange(0)
        pl.semaphore_wait(ready_sem, share - 1)

        @pl.when(speaks)
        def _():
            each((t + 1) * share, R, lambda rr: b_copy(ybuf, rr).start())

        @pl.when(t == 0)
        def _():
            each(1, C // per, lambda tt: y_copy(tt).start())
            prepare(upper, 1)

    @pl.when(jnp.logical_not(solver))
    def _():
        pl.semaphore_wait(ready_sem, share - 1)
        got = []
        for i in range(pieces):
            remote(ybuf, bcast.at[i], bsend_sem.at[0], brecv_sem.at[i], (r, t * per)).wait_recv()
            got.append(bcast[i])
        value = product(complex_left(got, nvec), fac_hi[...], fac_lo[...], dot_nt)
        vbuf[...] = value
        v_each(lambda copy: copy.start())
        vrecv[c] = value

    @pl.when(j == 0)
    def _():
        prepare_basis()
        side_work()

    @pl.when(t == 0)
    def _():
        @pl.when(jnp.logical_not(solver))
        def _():
            remote(ybuf, ybuf, ysend_sem.at[0], yrecv_sem.at[0], (r, h)).wait_recv()

        g = v_sum(per, C, ybuf[...])
        send_first(g, lead_hi[...], lead_lo[...])
        xbuf[...] = solve(1, g)

    @pl.when(t > 0)
    def _():
        @pl.when(solver)
        def _():
            xbuf[...] = solve(1, v_sum((t + 1) * per, C, ybuf[...]))

            @pl.when(speaks)
            def _():
                each(0, t * share, lambda rr: b_copy(xbuf, rr).start())

            each(0, t, lambda tt: x_copy(tt).start())
            each(t + 1, C // per, lambda tt: x_copy(tt).start())

        @pl.when(jnp.logical_not(solver))
        def _():
            remote(ybuf, xbuf, xsend_sem.at[0], xrecv_sem.at[0], (r, t * per)).wait_recv()

        send_first(xbuf[...], bas_hi[...], bas_lo[...])

    frecv[r] = fsend[...]

    def f_wait(d):
        q = (r + d) % R
        remote(fsend, frecv.at[q], fsend_sem.at[d], frecv_sem.at[q], (q, c)).wait_recv()

    each(1, R, f_wait)
    first = frecv[0]
    for i in range(1, R):
        first = first + frecv[i]
    ends = product(first, end_hi[...], end_lo[...], dot_nn)
    coefficients[0] = ends[:, :nb]
    coefficients[1] = ends[:, nb:2 * nb]
    projected[0] = xbuf[:nvec] - ends[:, 2 * nb:2 * nb + rows]
    projected[1] = xbuf[nvec:] - ends[:, 2 * nb + rows:]

    each(1, R, lambda d: f_copy(d).wait_send())
    for i in range(steps):
        gram_copy(i).wait_send()

    def parts_sent(sweep):
        for d in range(1, share):
            part_copy(sweep, d).wait_send()

    @pl.when(t == 0)
    def _():
        parts_sent(1)
        for d in range(1, share):
            t_copy(d).wait_send()

    @pl.when(solver)
    def _():
        parts_sent(0)

        @pl.when(speaks)
        def _():
            each((t + 1) * share, R, lambda rr: b_copy(ybuf, rr).wait_send())

        @pl.when(t == 0)
        def _():
            each(1, C // per, lambda tt: y_copy(tt).wait_send())

        @pl.when(t > 0)
        def _():
            parts_sent(1)

            @pl.when(speaks)
            def _():
                each(0, t * share, lambda rr: b_copy(xbuf, rr).wait_send())

            each(0, t, lambda tt: x_copy(tt).wait_send())
            each(t + 1, C // per, lambda tt: x_copy(tt).wait_send())

    @pl.when(jnp.logical_not(solver))
    def _():
        v_each(lambda copy: copy.wait_send())


def finish(projected, turned, projected_out, turned_out):
    projected_out[...] = projected[...]
    turned_out[...] = turned[...]


def local(R, C, factor, lower, upper, krylov, basis):
    tile, rows = lower.shape[1], lower.shape[2]
    width = factor.shape[2]
    nvec, nb = krylov.shape[1], basis.shape[1]
    share, per, pieces = tile // rows, tile // width, width // rows
    steps = R.bit_length() - 1
    dma = pltpu.SemaphoreType.DMA
    vmem = pl.BlockSpec(memory_space=pltpu.VMEM)
    block = (2 * nvec, rows)
    projected, turned = pl.pallas_call(
        functools.partial(kernel, R, C),
        out_shape=(
            jax.ShapeDtypeStruct(krylov.shape, F32),
            jax.ShapeDtypeStruct((2, nvec, nb), F32),
        ),
        in_specs=[vmem] * 5,
        out_specs=(vmem, vmem),
        scratch_shapes=[
            pltpu.VMEM((2, tile, 2 * rows), BF16),
            pltpu.VMEM((2, tile, 2 * rows), BF16),
            pltpu.VMEM((rows, 2 * width), BF16),
            pltpu.VMEM((rows, 2 * width), BF16),
            pltpu.VMEM((2 * nb, 2 * rows), BF16),
            pltpu.VMEM((2 * nb, 2 * rows), BF16),
            pltpu.VMEM((2 * nb, 2 * nb + 2 * rows), BF16),
            pltpu.VMEM((2 * nb, 2 * nb + 2 * rows), BF16),
            pltpu.VMEM((2 * nb, 2 * rows), BF16),
            pltpu.VMEM((2 * nb, 2 * rows), BF16),
            pltpu.VMEM((share, 2, nb, rows), F32),
            pltpu.VMEM((2, share) + block, F32),
            pltpu.VMEM((2, share) + block, F32),
            pltpu.VMEM(block, F32),
            pltpu.VMEM(block, F32),
            pltpu.VMEM((pieces,) + block, F32),
            pltpu.VMEM(block, F32),
            pltpu.VMEM((C,) + block, F32),
            pltpu.VMEM((nvec, 2 * nb), F32),
            pltpu.VMEM((R, nvec, 2 * nb), F32),
            pltpu.VMEM((steps + 1, nb, 2 * nb), F32),
            pltpu.VMEM((steps, nb, 2 * nb), F32),
            dma((2, share)),
            dma((2, share)),
            dma((R,)),
            dma((pieces,)),
            dma((C,)),
            dma((C,)),
            dma((C // per,)),
            dma((1,)),
            dma((R,)),
            dma((R,)),
            dma((steps,)),
            dma((steps,)),
            dma((share,)),
            dma((share,)),
            dma((C // per,)),
            dma((1,)),
            pltpu.SemaphoreType.REGULAR,
        ],
        compiler_params=pltpu.CompilerParams(collective_id=0, has_side_effects=True),
        name="krylov_step",
    )(factor, lower, upper, krylov, basis)
    projected, turned = pl.pallas_call(
        finish,
        out_shape=(jax.ShapeDtypeStruct(projected.shape, F32), jax.ShapeDtypeStruct(turned.shape, F32)),
        in_specs=[vmem] * 2,
        out_specs=(vmem, vmem),
        name="finish",
    )(projected, turned)
    return projected, turned.transpose(0, 2, 1)


def solution(mesh):
    in_specs = (
        P(None, "row", "col"),
        P(None, None, "row"),
        P(None, None, "row"),
        P(None, None, "row"),
        P(None, None, "row"),
    )
    out_specs = (P(None, None, "row"), P())
    body = functools.partial(local, mesh.shape["row"], mesh.shape["col"])
    return jax.shard_map(body, mesh=mesh, in_specs=in_specs, out_specs=out_specs, check_vma=False)
```

profile of v0, /device:TPU:0, one launch (start us, length us, event | category | flops | bytes accessed | tf_op | source)
XLA Modules:
  0.0 37.9 jit_solution(8263793176259493580)
XLA Ops:
  0.6 35.9 %krylov_step.1 = (f32[2,16,128]{2,1,0:T(8,128)}, f32[2,16,64]{2,1,0:T(8,128)}) custom-call(f32[2,128,256]{2,1,0:T(8,128)} %factor.1, f32[2,512,128]{2,1,0:T(8,128)} %lower.1, f32[2,512,128]{2,1,0:T(8,128)} %upper.1, f32[2,16,128]{2,1,0:T(8,128)} %krylov.1, f32[2,64,128]{2,1,0:T(8,128)} %basis.1), custom_call_target="tpu_custom_call" | custom-call | tf_op jit(solution)/shard_map/krylov_step/pallas_call | solution.py:405
  36.6 1.3 %finish.1 = (f32[2,16,128]{2,1,0:T(8,128)}, f32[2,16,64]{2,1,0:T(8,128)}) custom-call(f32[2,16,128]{2,1,0:T(8,128)} %get-tuple-element.6.projected, f32[2,16,64]{2,1,0:T(8,128)} %get-tuple-element.7.turned), custom_call_target="tpu_custom_call" | custom-call | tf_op jit(solution)/shard_map/finish/pallas_call | solution.py:457
where the time goes:
time: 38.1 us; the launch traced here: 37.9 us
  Pallas kernels  37.3 us (98%)
  between operations  0.64 us (2%)
    pallas_call x1, Pallas kernels, local(): pl.pallas_call(functools.partial(kernel, R, C), out_shape=(jax.ShapeDtype...  35.9 us
    pallas_call x1, Pallas kernels, local(): pl.pallas_call(finish, out_shape=(jax.ShapeDtypeStruct(projected.shape, F...  1.35 us

commit v1 on v0

--- a/solution.py
+++ b/solution.py
@@ -388,12 +388,479 @@
         v_each(lambda copy: copy.wait_send())
 
 
+def hub_kernel(
+    R, C, factor, lower, upper, krylov, basis, projected, coefficients,
+    fac_in, low_in, up_in, kry_in, bas_in, up_recv, f_recv,
+    low_hi, low_lo, up_hi, up_lo, fac_hi, fac_lo, lead_hi, lead_lo,
+    bas_hi, bas_lo, end_hi, end_lo, gather, gather_one,
+    asend, arecv, ybuf, yrecv, dsend, drecv, esend, erecv, xrecv,
+    fsend, frecv, gacc, grecv,
+    load_sem, asend_sem, arecv_sem, ysend_sem, yrecv_sem, dsend_sem, drecv_sem,
+    esend_sem, erecv_sem, xsend_sem, xrecv_sem, fsend_sem, frecv_sem,
+    usend_sem, urecv_sem, msend_sem, mrecv_sem, tsend_sem, trecv_sem, osend_sem, orecv_sem,
+    gsend_sem, grecv_sem, hsend_sem, hrecv_sem,
+):
+    tile, rows = lower.shape[1], lower.shape[2]
+    width = factor.shape[2]
+    nvec = krylov.shape[1]
+    nb = basis.shape[1]
+    share = tile // rows
+    per = tile // width
+    half = share // 2
+    steps = R.bit_length() - 1
+    r = lax.axis_index("row")
+    c = lax.axis_index("col")
+    me = r * C + c
+    t, p = r // share, r % share
+    y, z = p % half, p // half
+    lead = per - 1
+    main = c == lead
+    hub = main & (z == 1 - t)
+    side = c == 0
+
+    def remote(src, dst, send, recv, dest):
+        return pltpu.make_async_remote_copy(
+            src_ref=src, dst_ref=dst, send_sem=send, recv_sem=recv, device_id=dest, device_id_type=MESH
+        )
+
+    def load(i, src, dst):
+        return pltpu.make_async_copy(src, dst, load_sem.at[i])
+
+    loads = [
+        load(0, lower, low_in), load(1, krylov, kry_in), load(2, factor, fac_in), load(3, upper, up_in),
+        load(4, basis, bas_in),
+    ]
+
+    @pl.when(main)
+    def _():
+        for i in range(4):
+            loads[i].start()
+
+    loads[4].start()
+
+    barrier = pltpu.get_barrier_semaphore()
+
+    def greet(i, carry):
+        other = (me + 1 + i) % (R * C)
+        pl.semaphore_signal(barrier, inc=1, device_id=(other // C, other % C), device_id_type=MESH)
+        return carry
+
+    lax.fori_loop(0, R * C - 1, greet, 0)
+
+    def when(cond):
+        return pl.when(cond)
+
+    def pair(ref, axis=1):
+        return jnp.concatenate([ref[0], ref[1]], axis)
+
+    def a_copy(d):
+        q = (p + d) % share
+        return remote(asend.at[q], arecv.at[p], asend_sem.at[q], arecv_sem.at[p], (t * share + q, c))
+
+    def a_wait(d):
+        q = (p + d) % share
+        remote(asend.at[q], arecv.at[q], asend_sem.at[q], arecv_sem.at[q], (t * share + q, c)).wait_recv()
+        return q
+
+    def y_copy(i):
+        return remote(ybuf, yrecv.at[p], ysend_sem.at[i], yrecv_sem.at[p], (share + i, c))
+
+    def y_hub():
+        return remote(ybuf, yrecv.at[p], ysend_sem.at[share], yrecv_sem.at[p], (half + y, c))
+
+    def y_wait(q):
+        remote(ybuf, yrecv.at[q], ysend_sem.at[0], yrecv_sem.at[q], ((r + 1) % R, c)).wait_recv()
+
+    def u_copy():
+        return remote(upper, up_recv, usend_sem.at[0], urecv_sem.at[0], (t * share + (1 - z) * half + y, c))
+
+    def m_near():
+        return remote(factor, f_recv.at[0, 0], msend_sem.at[0], mrecv_sem.at[0], (r, lead))
+
+    def m_far():
+        h = c % per
+        return remote(factor, f_recv.at[z, h], msend_sem.at[0], mrecv_sem.at[z * per + h], (half + y, lead))
+
+    def m_wait(zz, h):
+        remote(factor, f_recv.at[zz, h], msend_sem.at[0], mrecv_sem.at[zz * per + h], ((r + 1) % R, c)).wait_recv()
+
+    def t_copy(i):
+        return remote(basis, gather.at[p], tsend_sem.at[i], trecv_sem.at[p], (half + i, lead))
+
+    def t_wait(q):
+        remote(basis, gather.at[q], tsend_sem.at[0], trecv_sem.at[q], ((r + 1) % R, c)).wait_recv()
+
+    def o_copy():
+        return remote(basis, gather_one.at[z], osend_sem.at[0], orecv_sem.at[z], (half + y, lead))
+
+    def o_wait(zz):
+        remote(basis, gather_one.at[zz], osend_sem.at[0], orecv_sem.at[zz], ((r + 1) % R, c)).wait_recv()
+
+    def d_copy(i):
+        return remote(dsend.at[i], drecv.at[p], dsend_sem.at[i], drecv_sem.at[p], (share + i, c))
+
+    def d_wait(q):
+        remote(dsend.at[0], drecv.at[q], dsend_sem.at[0], drecv_sem.at[q], ((r + 1) % R, c)).wait_recv()
+
+    def e_copy(i):
+        return remote(esend, erecv.at[y], esend_sem.at[i], erecv_sem.at[y], (half + i, c))
+
+    def e_wait(i):
+        remote(esend, erecv.at[i], esend_sem.at[0], erecv_sem.at[i], ((r + 1) % R, c)).wait_recv()
+
+    def x_copy(i):
+        k, cc = i // C, i % C
+        return remote(esend.at[k], xrecv.at[y], xsend_sem.at[i], xrecv_sem.at[y], (t * share + k, cc))
+
+    def x_wait(i):
+        remote(esend.at[0], xrecv.at[i], xsend_sem.at[0], xrecv_sem.at[i], ((r + 1) % R, c)).wait_recv()
+
+    def f_copy(i):
+        return remote(fsend, frecv.at[y], fsend_sem.at[i], frecv_sem.at[y], (i // C, i % C))
+
+    def f_wait(i):
+        remote(fsend, frecv.at[i], fsend_sem.at[0], frecv_sem.at[i], ((r + 1) % R, c)).wait_recv()
+
+    def g_copy(i):
+        other = r + (1 << i) * (1 - 2 * ((r // (1 << i)) % 2))
+        return remote(gacc.at[i], grecv.at[i], gsend_sem.at[i], grecv_sem.at[i], (other, c))
+
+    def h_copy(cc):
+        return remote(gacc.at[steps], grecv.at[steps], hsend_sem.at[cc], hrecv_sem.at[0], (r, cc))
+
+    def each(first_index, last_index, act, skip=None):
+        def body(i, carry):
+            if skip is None:
+                act(i)
+            else:
+                @pl.when(i != skip)
+                def _():
+                    act(i)
+            return carry
+
+        lax.fori_loop(first_index, last_index, body, 0)
+
+    def store(hi, lo, index, value):
+        high, low = split(value)
+        hi[index] = high
+        lo[index] = low
+
+    def wide(value):
+        return jnp.concatenate([value[:nvec], value[nvec:]], 1)
+
+    def start_sends():
+        @when(side & (t == 1))
+        def _():
+            m_near().start()
+
+        @when((c >= per) & (t == 0))
+        def _():
+            m_far().start()
+
+        @when(main & jnp.logical_not(hub))
+        def _():
+            u_copy().start()
+
+        @when(main & (t == 0))
+        def _():
+            each(0, half, lambda i: t_copy(i).start(), jnp.where(z == 1, y, half))
+
+        @when(main & (t == 1))
+        def _():
+            o_copy().start()
+
+    def put_slices(ref, out):
+        for k in range(share):
+            ref[k] = out[:, k * rows:(k + 1) * rows]
+
+    def inverse_times(hi, lo, values):
+        left = jnp.concatenate([complex_left([v], nvec) for v in values], 1)
+        return product(left, hi, lo, dot_nt)
+
+    def factor_times(values, count):
+        left = jnp.concatenate(
+            [complex_left(values[h * half:(h + 1) * half], nvec) for h in range(per)], 1
+        )
+        return product(left, fac_hi[:count], fac_lo[:count], dot_nt)
+
+    span = 2 * rows
+    broad = 2 * width
+
+    @when(main & (t == 0))
+    def _():
+        loads[0].wait()
+        loads[1].wait()
+        store(low_hi, low_lo, ..., pair(low_in))
+        put_slices(asend, inverse_times(low_hi[...], low_lo[...], [pair(kry_in, 0)]))
+
+    pl.semaphore_wait(barrier, R * C - 1)
+
+    @when(main & (t == 0))
+    def _():
+        for d in range(1, share):
+            a_copy(d).start()
+
+    start_sends()
+
+    @when(main & (t == 0))
+    def _():
+        total = asend[p]
+        for d in range(1, share):
+            q = a_wait(d)
+            total = total + arecv[q]
+        ybuf[...] = total
+        for i in range(share - 1, -1, -1):
+            y_copy(i).start()
+
+        @when(z == 0)
+        def _():
+            y_hub().start()
+
+        loads[2].wait()
+        loads[3].wait()
+
+    loads[4].wait()
+
+    def prepare_basis():
+        top = pair(bas_in)
+        bottom = jnp.concatenate([-bas_in[1], bas_in[0]], 1)
+        store(bas_hi, bas_lo, ..., jnp.concatenate([top, bottom], 0))
+        return top
+
+    def prepare_end(top):
+        gram = jnp.concatenate([top, jnp.concatenate([-top[:, nb:], top[:, :nb]], 1)], 0)
+        row_id = lax.broadcasted_iota(jnp.int32, gram.shape, 0)
+        col_id = lax.broadcasted_iota(jnp.int32, gram.shape, 1)
+        twice = jnp.where(row_id == col_id, 2.0, 0.0) - gram
+        spread = product(twice, bas_hi[...], bas_lo[...], dot_nn)
+        store(end_hi, end_lo, ..., jnp.concatenate([twice, spread], 1))
+
+    def end_from_side():
+        prepare_basis()
+        remote(gacc.at[0], grecv.at[steps], hsend_sem.at[0], hrecv_sem.at[0], (r, 0)).wait_recv()
+        prepare_end(grecv[steps])
+
+    @when(side)
+    def _():
+        gacc[0] = product(prepare_basis(), bas_hi[...], bas_lo[...], dot_nt)
+        for i in range(steps):
+            copy = g_copy(i)
+            copy.start()
+            copy.wait_recv()
+            gacc[i + 1] = gacc[i] + grecv[i]
+        each(1, C, lambda cc: h_copy(cc).start())
+        prepare_end(gacc[steps])
+
+    @when(c > lead)
+    def _():
+        end_from_side()
+
+    @when(main & (t == 1))
+    def _():
+        for i in range(4):
+            loads[i].wait()
+        store(low_hi, low_lo, ..., pair(low_in))
+        store(fac_hi, fac_lo, (slice(0, rows), slice(broad, 2 * broad)), pair(fac_in))
+        m_wait(0, 0)
+        store(fac_hi, fac_lo, (slice(0, rows), slice(0, broad)), pair(f_recv.at[0, 0]))
+
+        @when(hub)
+        def _():
+            store(up_hi, up_lo, (slice(None), slice(0, span)), pair(up_in))
+
+        for q in range(share):
+            y_wait(q)
+        g = pair(kry_in, 0) - factor_times([yrecv[q] for q in range(share)], rows)
+        out = inverse_times(low_hi[...], low_lo[...], [g])
+        for i in range(half):
+            for k in range(2):
+                dsend[i, k] = out[:, (k * half + i) * rows:(k * half + i + 1) * rows]
+        each(0, half, lambda i: d_copy(i).start(), jnp.where(hub, y, half))
+
+        @when(hub)
+        def _():
+            drecv[p] = dsend[y]
+            remote(upper, up_recv, usend_sem.at[0], urecv_sem.at[0], ((r + 1) % R, c)).wait_recv()
+            store(up_hi, up_lo, (slice(None), slice(span, 2 * span)), pair(up_recv))
+
+            each(0, share, d_wait, p)
+            parts = [drecv[q] for q in range(share)]
+            total = (parts[0] + parts[1]) + (parts[2] + parts[3])
+            put_slices(esend, inverse_times(up_hi[...], up_lo[...], [total[0], total[1]]))
+            for i in range(half):
+                e_copy(i).start()
+            each(0, share * C, lambda i: x_copy(i).start(), p * C + c)
+            xrecv[y] = esend[p]
+
+        end_from_side()
+
+    @when(main & (t == 0))
+    def _():
+        @when(hub)
+        def _():
+            store(up_hi, up_lo, (slice(None), slice(span, 2 * span)), pair(up_in))
+            gather[p] = bas_in[...]
+            each(0, share, t_wait, p)
+            each(0, 2, o_wait)
+            stacked = jnp.concatenate(
+                [jnp.concatenate([gather[q, i] for q in range(share)], 1) for i in range(2)], 0
+            )
+            for k in range(2):
+                one = gather_one[k]
+                high, low = split(jnp.concatenate([
+                    jnp.concatenate([one[0], one[1]], 1), jnp.concatenate([-one[1], one[0]], 1)
+                ], 0))
+                at = slice((2 + k) * span, (3 + k) * span)
+                lead_hi[:, at] = high
+                lead_lo[:, at] = low
+            end_from_side()
+            remote(upper, up_recv, usend_sem.at[0], urecv_sem.at[0], ((r + 1) % R, c)).wait_recv()
+            store(up_hi, up_lo, (slice(None), slice(0, span)), pair(up_recv))
+            for k in range(2):
+                at = slice(k * span, (k + 1) * span)
+                out = product(stacked, up_hi[:, at], up_lo[:, at], dot_nn)
+                one = out[:nb, :rows] + out[nb:, rows:]
+                two = out[nb:, :rows] - out[:nb, rows:]
+                store(lead_hi, lead_lo, (slice(None), at), jnp.concatenate(
+                    [jnp.concatenate([one, two], 1), jnp.concatenate([-two, one], 1)], 0
+                ))
+            for k in range(2):
+                for h in range(per):
+                    m_wait(k, h)
+                    store(
+                        fac_hi, fac_lo, (slice(k * rows, (k + 1) * rows), slice(h * broad, (h + 1) * broad)),
+                        pair(f_recv.at[k, h]),
+                    )
+            y_wait(y)
+            yrecv[half + y] = ybuf[...]
+
+            for i in range(half):
+                e_wait(i)
+            x = [erecv[0, k] + erecv[1, k] for k in range(share)]
+            out = factor_times(x, 2 * rows)
+            w = [yrecv[k * half + y] - out[:, k * rows:(k + 1) * rows] for k in range(2)]
+            mine = [jnp.where(y == 0, x[k * half], x[k * half + 1]) for k in range(2)]
+            fsend[...] = product(
+                jnp.concatenate([wide(v) for v in w + mine], 1), lead_hi[...], lead_lo[...], dot_nt
+            )
+            each(0, R * C, lambda i: f_copy(R * C - 1 - i).start(), R * C - 1 - me)
+            frecv[y] = fsend[...]
+            put_slices(esend, inverse_times(up_hi[...], up_lo[...], w))
+            each(0, share * C, lambda i: x_copy(i).start(), p * C + c)
+            xrecv[y] = esend[p]
+
+        @when(jnp.logical_not(hub))
+        def _():
+            end_from_side()
+
+    each(0, half, f_wait, jnp.where(hub & (t == 0), y, half))
+    first = frecv[0] + frecv[1]
+    ends = product(first, end_hi[...], end_lo[...], dot_nn)
+    coefficients[0] = ends[:, :nb]
+    coefficients[1] = ends[:, nb:2 * nb]
+    each(0, half, x_wait, jnp.where(hub, y, half))
+    x = xrecv[0] + xrecv[1]
+    projected[0] = x[:nvec] - ends[:, 2 * nb:2 * nb + rows]
+    projected[1] = x[nvec:] - ends[:, 2 * nb + rows:]
+
+    @when(side)
+    def _():
+        for i in range(steps):
+            g_copy(i).wait_send()
+        each(1, C, lambda cc: h_copy(cc).wait_send())
+
+        @when(t == 1)
+        def _():
+            m_near().wait_send()
+
+    @when((c >= per) & (t == 0))
+    def _():
+        m_far().wait_send()
+
+    @when(main)
+    def _():
+        @when(jnp.logical_not(hub))
+        def _():
+            u_copy().wait_send()
+
+        @when(t == 0)
+        def _():
+            each(0, half, lambda i: t_copy(i).wait_send(), jnp.where(z == 1, y, half))
+            for d in range(1, share):
+                a_copy(d).wait_send()
+            for i in range(share):
+                y_copy(i).wait_send()
+
+            @when(z == 0)
+            def _():
+                y_hub().wait_send()
+
+        @when(t == 1)
+        def _():
+            o_copy().wait_send()
+            each(0, half, lambda i: d_copy(i).wait_send(), jnp.where(hub, y, half))
+
+        @when(hub)
+        def _():
+            each(0, share * C, lambda i: x_copy(i).wait_send(), p * C + c)
+
+            @when(t == 1)
+            def _():
+                for i in range(half):
+                    e_copy(i).wait_send()
+
+            @when(t == 0)
+            def _():
+                each(0, R * C, lambda i: f_copy(i).wait_send(), me)
+
+
+def hub_call(R, C, factor, lower, upper, krylov, basis):
+    tile, rows = lower.shape[1], lower.shape[2]
+    width = factor.shape[2]
+    nvec, nb = krylov.shape[1], basis.shape[1]
+    share, per = tile // rows, tile // width
+    half = share // 2
+    steps = R.bit_length() - 1
+    dma = pltpu.SemaphoreType.DMA
+    vmem = pl.BlockSpec(memory_space=pltpu.VMEM)
+    block = (2 * nvec, rows)
+    f32 = lambda *shape: pltpu.VMEM(shape, F32)
+    bf16 = lambda *shape: [pltpu.VMEM(shape, BF16)] * 2
+    return pl.pallas_call(
+        functools.partial(hub_kernel, R, C),
+        out_shape=(
+            jax.ShapeDtypeStruct(krylov.shape, F32),
+            jax.ShapeDtypeStruct((2, nvec, nb), F32),
+        ),
+        in_specs=[pl.BlockSpec(memory_space=pl.ANY)] * 5,
+        out_specs=(vmem, vmem),
+        scratch_shapes=[
+            f32(*factor.shape), f32(*lower.shape), f32(*upper.shape), f32(*krylov.shape), f32(*basis.shape),
+            f32(*upper.shape), f32(2, per, *factor.shape),
+            *bf16(tile, 2 * rows), *bf16(tile, 4 * rows), *bf16(2 * rows, 2 * tile), *bf16(2 * nb, 8 * rows),
+            *bf16(2 * nb, 2 * rows), *bf16(2 * nb, 2 * nb + 2 * rows),
+            f32(share, *basis.shape), f32(2, *basis.shape),
+            f32(share, *block), f32(share, *block), f32(*block), f32(share, *block),
+            f32(half, 2, *block), f32(share, 2, *block), f32(share, *block), f32(2, share, *block),
+            f32(half, *block), f32(nvec, 2 * nb), f32(half, nvec, 2 * nb),
+            f32(steps + 1, nb, 2 * nb), f32(steps + 1, nb, 2 * nb),
+            dma((5,)), dma((share,)), dma((share,)), dma((share + 1,)), dma((share,)),
+            dma((half,)), dma((share,)), dma((half,)), dma((half,)),
+            dma((share * C,)), dma((half,)), dma((R * C,)), dma((half,)),
+            dma((1,)), dma((1,)), dma((1,)), dma((2 * per,)), dma((half,)), dma((share,)), dma((1,)), dma((2,)),
+            dma((steps,)), dma((steps,)), dma((C,)), dma((1,)),
+        ],
+        compiler_params=pltpu.CompilerParams(collective_id=0, has_side_effects=True),
+        name="krylov_hubs",
+    )(factor, lower, upper, krylov, basis)
+
+
 def finish(projected, turned, projected_out, turned_out):
     projected_out[...] = projected[...]
     turned_out[...] = turned[...]
 
 
-def local(R, C, factor, lower, upper, krylov, basis):
+def general_call(R, C, factor, lower, upper, krylov, basis):
     tile, rows = lower.shape[1], lower.shape[2]
     width = factor.shape[2]
     nvec, nb = krylov.shape[1], basis.shape[1]
@@ -402,7 +869,7 @@
     dma = pltpu.SemaphoreType.DMA
     vmem = pl.BlockSpec(memory_space=pltpu.VMEM)
     block = (2 * nvec, rows)
-    projected, turned = pl.pallas_call(
+    return pl.pallas_call(
         functools.partial(kernel, R, C),
         out_shape=(
             jax.ShapeDtypeStruct(krylov.shape, F32),
@@ -454,6 +921,15 @@
         compiler_params=pltpu.CompilerParams(collective_id=0, has_side_effects=True),
         name="krylov_step",
     )(factor, lower, upper, krylov, basis)
+
+
+def local(R, C, factor, lower, upper, krylov, basis):
+    tile, rows = lower.shape[1], lower.shape[2]
+    share, per = tile // rows, tile // factor.shape[2]
+    vmem = pl.BlockSpec(memory_space=pltpu.VMEM)
+    paired = R == 2 * share and C == 2 * per and share == 4 and per == 2
+    call = hub_call if paired else general_call
+    projected, turned = call(R, C, factor, lower, upper, krylov, basis)
     projected, turned = pl.pallas_call(
         finish,
         out_shape=(jax.ShapeDtypeStruct(projected.shape, F32), jax.ShapeDtypeStruct(turned.shape, F32)),

time: 38.1 us -> 34 us (0.89)
  Pallas kernels: 37.3 us -> 33.1 us
    pallas_call x1, Pallas kernels: 35.9 us -> 31.8 us  [hub_call(): pl.pallas_call(functools.partial(hub_kernel, R, C), out_shape=(jax.ShapeD...]
where the time goes in v1:
time: 34 us; the launch traced here: 33.8 us
  Pallas kernels  33.1 us (97%)
  between operations  0.64 us (2%)
    pallas_call x1, Pallas kernels, hub_call(): pl.pallas_call(functools.partial(hub_kernel, R, C), out_shape=(jax.ShapeD...  31.8 us
    pallas_call x1, Pallas kernels, local(): pl.pallas_call(finish, out_shape=(jax.ShapeDtypeStruct(projected.shape, F...  1.35 us

profile of v1, /device:TPU:0, one launch (start us, length us, event | category | flops | bytes accessed | tf_op | source)
XLA Modules:
  0.0 33.8 jit_solution(3996028013836167430)
XLA Ops:
  0.6 31.8 %krylov_hubs.1 = (f32[2,16,128]{2,1,0:T(8,128)}, f32[2,16,64]{2,1,0:T(8,128)}) custom-call(f32[2,128,256]{2,1,0:T(8,128)} %factor.1, f32[2,512,128]{2,1,0:T(8,128)} %lower.1, f32[2,512,128]{2,1,0:T(8,128)} %upper.1, f32[2,16,128]{2,1,0:T(8,128)} %krylov.1, f32[2,64,128]{2,1,0:T(8,128)} %basis.1), custom_call_target="tpu_custom_call" | custom-call | tf_op jit(solution)/shard_map/krylov_hubs/pallas_call | solution.py:829
  32.4 1.3 %finish.1 = (f32[2,16,128]{2,1,0:T(8,128)}, f32[2,16,64]{2,1,0:T(8,128)}) custom-call(f32[2,16,128]{2,1,0:T(8,128)} %get-tuple-element.6.projected, f32[2,16,64]{2,1,0:T(8,128)} %get-tuple-element.7.turned), custom_call_target="tpu_custom_call" | custom-call | tf_op jit(solution)/shard_map/finish/pallas_call | solution.py:933

commit v2 on v1

--- a/solution.py
+++ b/solution.py
@@ -398,7 +398,7 @@
     load_sem, asend_sem, arecv_sem, ysend_sem, yrecv_sem, dsend_sem, drecv_sem,
     esend_sem, erecv_sem, xsend_sem, xrecv_sem, fsend_sem, frecv_sem,
     usend_sem, urecv_sem, msend_sem, mrecv_sem, tsend_sem, trecv_sem, osend_sem, orecv_sem,
-    gsend_sem, grecv_sem, hsend_sem, hrecv_sem,
+    gsend_sem, grecv_sem, hsend_sem, hrecv_sem, next_sem, all_sem,
 ):
     tile, rows = lower.shape[1], lower.shape[2]
     width = factor.shape[2]
@@ -418,6 +418,9 @@
     hub = main & (z == 1 - t)
     side = c == 0
 
+    def partner(i):
+        return r + (1 << i) * (1 - 2 * ((r // (1 << i)) % 2))
+
     def remote(src, dst, send, recv, dest):
         return pltpu.make_async_remote_copy(
             src_ref=src, dst_ref=dst, send_sem=send, recv_sem=recv, device_id=dest, device_id_type=MESH
@@ -439,13 +442,61 @@
     loads[4].start()
 
     barrier = pltpu.get_barrier_semaphore()
-
-    def greet(i, carry):
-        other = (me + 1 + i) % (R * C)
-        pl.semaphore_signal(barrier, inc=1, device_id=(other // C, other % C), device_id_type=MESH)
-        return carry
-
-    lax.fori_loop(0, R * C - 1, greet, 0)
+    guide = (c == per) & (t == 0) & (z == 1)
+    far = (c >= per) & (t == 0)
+
+    def greet(rr, cc):
+        pl.semaphore_signal(barrier, inc=1, device_id=(rr, cc), device_id_type=MESH)
+
+    @pl.when(main)
+    def _():
+        for d in range(1, share):
+            greet(t * share + (p + d) % share, c)
+        greet(r, 0)
+
+        @pl.when(t == 1)
+        def _():
+            for q in range(share):
+                greet(q, 0)
+
+        @pl.when(hub & (t == 0))
+        def _():
+            greet(y, per)
+            for cc in range(per + 1, C):
+                greet(y, cc)
+                greet(r, cc)
+
+    @pl.when(side)
+    def _():
+        for i in range(steps):
+            greet(partner(i), c)
+
+    @pl.when(c >= per)
+    def _():
+        greet(r, 0)
+
+    for i in range(half):
+        @pl.when(jnp.logical_not(guide & (y == i)))
+        def _():
+            greet(half + i, per)
+
+    def arrive():
+        count = jnp.where(main, share - 1, jnp.where(
+            side, steps + 1 + C - per + jnp.where(t == 0, share, 0),
+            jnp.where(guide, R * C - 1, jnp.where(far, 1, 0)),
+        ))
+        @pl.when(main | side | far)
+        def _():
+            pl.semaphore_wait(barrier, count)
+
+        @pl.when(side & (t == 0))
+        def _():
+            pl.semaphore_signal(next_sem, inc=1, device_id=(r, lead), device_id_type=MESH)
+
+        @pl.when(guide)
+        def _():
+            for i in range(2):
+                pl.semaphore_signal(all_sem, inc=1, device_id=(half * (i + 1) + y, lead), device_id_type=MESH)
 
     def when(cond):
         return pl.when(cond)
@@ -521,9 +572,12 @@
     def f_wait(i):
         remote(fsend, frecv.at[i], fsend_sem.at[0], frecv_sem.at[i], ((r + 1) % R, c)).wait_recv()
 
+    def both(i):
+        x_copy(i).start()
+        f_copy(i).start()
+
     def g_copy(i):
-        other = r + (1 << i) * (1 - 2 * ((r // (1 << i)) % 2))
-        return remote(gacc.at[i], grecv.at[i], gsend_sem.at[i], grecv_sem.at[i], (other, c))
+        return remote(gacc.at[i], grecv.at[i], gsend_sem.at[i], grecv_sem.at[i], (partner(i), c))
 
     def h_copy(cc):
         return remote(gacc.at[steps], grecv.at[steps], hsend_sem.at[cc], hrecv_sem.at[0], (r, cc))
@@ -553,21 +607,13 @@
         def _():
             m_near().start()
 
-        @when((c >= per) & (t == 0))
+        @when(far)
         def _():
             m_far().start()
 
-        @when(main & jnp.logical_not(hub))
+        @when(main & (t == 1) & (z == 1))
         def _():
             u_copy().start()
-
-        @when(main & (t == 0))
-        def _():
-            each(0, half, lambda i: t_copy(i).start(), jnp.where(z == 1, y, half))
-
-        @when(main & (t == 1))
-        def _():
-            o_copy().start()
 
     def put_slices(ref, out):
         for k in range(share):
@@ -593,7 +639,7 @@
         store(low_hi, low_lo, ..., pair(low_in))
         put_slices(asend, inverse_times(low_hi[...], low_lo[...], [pair(kry_in, 0)]))
 
-    pl.semaphore_wait(barrier, R * C - 1)
+    arrive()
 
     @when(main & (t == 0))
     def _():
@@ -609,12 +655,19 @@
             q = a_wait(d)
             total = total + arecv[q]
         ybuf[...] = total
+        pl.semaphore_wait(next_sem, 1)
         for i in range(share - 1, -1, -1):
             y_copy(i).start()
 
         @when(z == 0)
         def _():
             y_hub().start()
+
+        each(0, half, lambda i: t_copy(i).start(), jnp.where(z == 1, y, half))
+
+        @when(z == 0)
+        def _():
+            u_copy().start()
 
         loads[2].wait()
         loads[3].wait()
@@ -676,6 +729,7 @@
             for k in range(2):
                 dsend[i, k] = out[:, (k * half + i) * rows:(k * half + i + 1) * rows]
         each(0, half, lambda i: d_copy(i).start(), jnp.where(hub, y, half))
+        o_copy().start()
 
         @when(hub)
         def _():
@@ -689,6 +743,7 @@
             put_slices(esend, inverse_times(up_hi[...], up_lo[...], [total[0], total[1]]))
             for i in range(half):
                 e_copy(i).start()
+            pl.semaphore_wait(all_sem, 1)
             each(0, share * C, lambda i: x_copy(i).start(), p * C + c)
             xrecv[y] = esend[p]
 
@@ -701,19 +756,9 @@
             store(up_hi, up_lo, (slice(None), slice(span, 2 * span)), pair(up_in))
             gather[p] = bas_in[...]
             each(0, share, t_wait, p)
-            each(0, 2, o_wait)
             stacked = jnp.concatenate(
                 [jnp.concatenate([gather[q, i] for q in range(share)], 1) for i in range(2)], 0
             )
-            for k in range(2):
-                one = gather_one[k]
-                high, low = split(jnp.concatenate([
-                    jnp.concatenate([one[0], one[1]], 1), jnp.concatenate([-one[1], one[0]], 1)
-                ], 0))
-                at = slice((2 + k) * span, (3 + k) * span)
-                lead_hi[:, at] = high
-                lead_lo[:, at] = low
-            end_from_side()
             remote(upper, up_recv, usend_sem.at[0], urecv_sem.at[0], ((r + 1) % R, c)).wait_recv()
             store(up_hi, up_lo, (slice(None), slice(0, span)), pair(up_recv))
             for k in range(2):
@@ -733,6 +778,16 @@
                     )
             y_wait(y)
             yrecv[half + y] = ybuf[...]
+            each(0, 2, o_wait)
+            for k in range(2):
+                one = gather_one[k]
+                high, low = split(jnp.concatenate([
+                    jnp.concatenate([one[0], one[1]], 1), jnp.concatenate([-one[1], one[0]], 1)
+                ], 0))
+                at = slice((2 + k) * span, (3 + k) * span)
+                lead_hi[:, at] = high
+                lead_lo[:, at] = low
+            pl.semaphore_wait(all_sem, 1)
 
             for i in range(half):
                 e_wait(i)
@@ -740,14 +795,15 @@
             out = factor_times(x, 2 * rows)
             w = [yrecv[k * half + y] - out[:, k * rows:(k + 1) * rows] for k in range(2)]
             mine = [jnp.where(y == 0, x[k * half], x[k * half + 1]) for k in range(2)]
+            put_slices(esend, inverse_times(up_hi[...], up_lo[...], w))
             fsend[...] = product(
                 jnp.concatenate([wide(v) for v in w + mine], 1), lead_hi[...], lead_lo[...], dot_nt
             )
-            each(0, R * C, lambda i: f_copy(R * C - 1 - i).start(), R * C - 1 - me)
+            each(0, share * C, lambda i: both(i), p * C + c)
+            each(share * C, R * C, lambda i: f_copy(i).start())
+            xrecv[y] = esend[p]
             frecv[y] = fsend[...]
-            put_slices(esend, inverse_times(up_hi[...], up_lo[...], w))
-            each(0, share * C, lambda i: x_copy(i).start(), p * C + c)
-            xrecv[y] = esend[p]
+            end_from_side()
 
         @when(jnp.logical_not(hub))
         def _():
@@ -828,10 +884,7 @@
     bf16 = lambda *shape: [pltpu.VMEM(shape, BF16)] * 2
     return pl.pallas_call(
         functools.partial(hub_kernel, R, C),
-        out_shape=(
-            jax.ShapeDtypeStruct(krylov.shape, F32),
-            jax.ShapeDtypeStruct((2, nvec, nb), F32),
-        ),
+        out_shape=(pltpu.VMEM(krylov.shape, F32), pltpu.VMEM((2, nvec, nb), F32)),
         in_specs=[pl.BlockSpec(memory_space=pl.ANY)] * 5,
         out_specs=(vmem, vmem),
         scratch_shapes=[
@@ -849,15 +902,22 @@
             dma((share * C,)), dma((half,)), dma((R * C,)), dma((half,)),
             dma((1,)), dma((1,)), dma((1,)), dma((2 * per,)), dma((half,)), dma((share,)), dma((1,)), dma((2,)),
             dma((steps,)), dma((steps,)), dma((C,)), dma((1,)),
+            pltpu.SemaphoreType.REGULAR, pltpu.SemaphoreType.REGULAR,
         ],
         compiler_params=pltpu.CompilerParams(collective_id=0, has_side_effects=True),
         name="krylov_hubs",
     )(factor, lower, upper, krylov, basis)
 
 
-def finish(projected, turned, projected_out, turned_out):
-    projected_out[...] = projected[...]
-    turned_out[...] = turned[...]
+def finish(projected, turned, projected_out, turned_out, sems):
+    copies = [
+        pltpu.make_async_copy(projected, projected_out, sems.at[0]),
+        pltpu.make_async_copy(turned, turned_out, sems.at[1]),
+    ]
+    for copy in copies:
+        copy.start()
+    for copy in copies:
+        copy.wait()
 
 
 def general_call(R, C, factor, lower, upper, krylov, basis):
@@ -930,11 +990,14 @@
     paired = R == 2 * share and C == 2 * per and share == 4 and per == 2
     call = hub_call if paired else general_call
     projected, turned = call(R, C, factor, lower, upper, krylov, basis)
+    if paired:
+        projected, turned = [pltpu.with_memory_space_constraint(x, pltpu.VMEM) for x in (projected, turned)]
     projected, turned = pl.pallas_call(
         finish,
         out_shape=(jax.ShapeDtypeStruct(projected.shape, F32), jax.ShapeDtypeStruct(turned.shape, F32)),
         in_specs=[vmem] * 2,
-        out_specs=(vmem, vmem),
+        out_specs=[pl.BlockSpec(memory_space=pl.ANY)] * 2,
+        scratch_shapes=[pltpu.SemaphoreType.DMA((2,))],
         name="finish",
     )(projected, turned)
     return projected, turned.transpose(0, 2, 1)

time: 34 us -> 23.4 us (0.69)
  Pallas kernels: 33.1 us -> 22.6 us
    pallas_call x1, Pallas kernels: 31.8 us -> 21.9 us  [hub_call(): pl.pallas_call(functools.partial(hub_kernel, R, C), out_shape=(pltpu.VMEM...]
    pallas_call x1, Pallas kernels: 1.35 us -> 0.63 us  [local(): pl.pallas_call(finish, out_shape=(jax.ShapeDtypeStruct(projected.shape, F...]
where the time goes in v2:
time: 23.4 us; the launch traced here: 23.2 us
  Pallas kernels  22.6 us (97%)
  between operations  0.64 us (3%)
    pallas_call x1, Pallas kernels, hub_call(): pl.pallas_call(functools.partial(hub_kernel, R, C), out_shape=(pltpu.VMEM...  21.9 us
    pallas_call x1, Pallas kernels, local(): pl.pallas_call(finish, out_shape=(jax.ShapeDtypeStruct(projected.shape, F...  0.63 us

profile of v2, /device:TPU:0, one launch (start us, length us, event | category | flops | bytes accessed | tf_op | source)
XLA Modules:
  0.0 23.2 jit_solution(4741859359891505445)
XLA Ops:
  0.6 21.9 %krylov_hubs.1 = (f32[2,16,128]{2,1,0:T(8,128)S(1)}, f32[2,16,64]{2,1,0:T(8,128)S(1)}) custom-call(f32[2,128,256]{2,1,0:T(8,128)} %factor.1, f32[2,512,128]{2,1,0:T(8,128)} %lower.1, f32[2,512,128]{2,1,0:T(8,128)} %upper.1, f32[2,16,128]{2,1,0:T(8,128)} %krylov.1, f32[2,64,128]{2,1,0:T(8,128)} %basis.1), custom_call_target="tpu_custom_call" | custom-call | tf_op jit(solution)/shard_map/krylov_hubs/pallas_call | solution.py:885
  22.6 0.6 %finish.1 = (f32[2,16,128]{2,1,0:T(8,128)}, f32[2,16,64]{2,1,0:T(8,128)}) custom-call(f32[2,16,128]{2,1,0:T(8,128)S(1)} %get-tuple-element.6.projected, f32[2,16,64]{2,1,0:T(8,128)S(1)} %get-tuple-element.7.turned), custom_call_target="tpu_custom_call" | custom-call | tf_op jit(solution)/shard_map/finish/pallas_call | solution.py:995

commit v3 on v2

--- a/solution.py
+++ b/solution.py
@@ -391,10 +391,9 @@
 def hub_kernel(
     R, C, factor, lower, upper, krylov, basis, projected, coefficients,
     fac_in, low_in, up_in, kry_in, bas_in, up_recv, f_recv,
-    low_hi, low_lo, up_hi, up_lo, fac_hi, fac_lo, lead_hi, lead_lo,
+    low_hi, low_lo, up_hi, up_lo, fac_hi, fac_lo,
     bas_hi, bas_lo, end_hi, end_lo, gather, gather_one,
-    asend, arecv, ybuf, yrecv, dsend, drecv, esend, erecv, xrecv,
-    fsend, frecv, gacc, grecv,
+    asend, arecv, ybuf, yrecv, dsend, drecv, esend, erecv, gsend, xrecv, gacc, grecv,
     load_sem, asend_sem, arecv_sem, ysend_sem, yrecv_sem, dsend_sem, drecv_sem,
     esend_sem, erecv_sem, xsend_sem, xrecv_sem, fsend_sem, frecv_sem,
     usend_sem, urecv_sem, msend_sem, mrecv_sem, tsend_sem, trecv_sem, osend_sem, orecv_sem,
@@ -414,6 +413,7 @@
     t, p = r // share, r % share
     y, z = p % half, p // half
     lead = per - 1
+    both = 2 * nvec
     main = c == lead
     hub = main & (z == 1 - t)
     side = c == 0
@@ -442,7 +442,7 @@
     loads[4].start()
 
     barrier = pltpu.get_barrier_semaphore()
-    guide = (c == per) & (t == 0) & (z == 1)
+    guide = (c == per) & (t == 1) & (z == 0)
     far = (c >= per) & (t == 0)
 
     def greet(rr, cc):
@@ -450,19 +450,21 @@
 
     @pl.when(main)
     def _():
-        for d in range(1, share):
-            greet(t * share + (p + d) % share, c)
+        @pl.when(hub)
+        def _():
+            for d in range(1, share):
+                greet(t * share + (p + d) % share, c)
+
         greet(r, 0)
 
         @pl.when(t == 1)
         def _():
-            for q in range(share):
-                greet(q, 0)
+            for i in range(half):
+                greet(half + i, 0)
 
         @pl.when(hub & (t == 0))
         def _():
-            greet(y, per)
-            for cc in range(per + 1, C):
+            for cc in range(per, C):
                 greet(y, cc)
                 greet(r, cc)
 
@@ -478,18 +480,18 @@
     for i in range(half):
         @pl.when(jnp.logical_not(guide & (y == i)))
         def _():
-            greet(half + i, per)
+            greet(share + i, per)
 
     def arrive():
-        count = jnp.where(main, share - 1, jnp.where(
-            side, steps + 1 + C - per + jnp.where(t == 0, share, 0),
+        count = jnp.where(main, jnp.where(hub, half - 1, half), jnp.where(
+            side, steps + 1 + C - per + jnp.where((t == 0) & (z == 1), share, 0),
             jnp.where(guide, R * C - 1, jnp.where(far, 1, 0)),
         ))
-        @pl.when(main | side | far)
+        @pl.when(main | side | far | guide)
         def _():
             pl.semaphore_wait(barrier, count)
 
-        @pl.when(side & (t == 0))
+        @pl.when(side & (t == 0) & (z == 1))
         def _():
             pl.semaphore_signal(next_sem, inc=1, device_id=(r, lead), device_id_type=MESH)
 
@@ -504,23 +506,19 @@
     def pair(ref, axis=1):
         return jnp.concatenate([ref[0], ref[1]], axis)
 
-    def a_copy(d):
-        q = (p + d) % share
-        return remote(asend.at[q], arecv.at[p], asend_sem.at[q], arecv_sem.at[p], (t * share + q, c))
-
-    def a_wait(d):
-        q = (p + d) % share
-        remote(asend.at[q], arecv.at[q], asend_sem.at[q], arecv_sem.at[q], (t * share + q, c)).wait_recv()
-        return q
+    def a_copy(i):
+        i = (y + 1 + i) % half
+        return remote(asend.at[i], arecv.at[p], asend_sem.at[i], arecv_sem.at[p], (half + i, c))
+
+    def a_wait(q):
+        remote(asend.at[0], arecv.at[q], asend_sem.at[0], arecv_sem.at[q], ((r + 1) % R, c)).wait_recv()
 
     def y_copy(i):
-        return remote(ybuf, yrecv.at[p], ysend_sem.at[i], yrecv_sem.at[p], (share + i, c))
-
-    def y_hub():
-        return remote(ybuf, yrecv.at[p], ysend_sem.at[share], yrecv_sem.at[p], (half + y, c))
-
-    def y_wait(q):
-        remote(ybuf, yrecv.at[q], ysend_sem.at[0], yrecv_sem.at[q], ((r + 1) % R, c)).wait_recv()
+        i = (1 - i // half) * half + (y + 1 + i) % half
+        return remote(ybuf, yrecv.at[y], ysend_sem.at[i], yrecv_sem.at[y], (share + i, c))
+
+    def y_wait(i):
+        remote(ybuf, yrecv.at[i], ysend_sem.at[0], yrecv_sem.at[i], ((r + 1) % R, c)).wait_recv()
 
     def u_copy():
         return remote(upper, up_recv, usend_sem.at[0], urecv_sem.at[0], (t * share + (1 - z) * half + y, c))
@@ -548,33 +546,48 @@
         remote(basis, gather_one.at[zz], osend_sem.at[0], orecv_sem.at[zz], ((r + 1) % R, c)).wait_recv()
 
     def d_copy(i):
+        i = (y + 1 + i) % half
         return remote(dsend.at[i], drecv.at[p], dsend_sem.at[i], drecv_sem.at[p], (share + i, c))
 
     def d_wait(q):
         remote(dsend.at[0], drecv.at[q], dsend_sem.at[0], drecv_sem.at[q], ((r + 1) % R, c)).wait_recv()
 
     def e_copy(i):
-        return remote(esend, erecv.at[y], esend_sem.at[i], erecv_sem.at[y], (half + i, c))
-
-    def e_wait(i):
-        remote(esend, erecv.at[i], esend_sem.at[0], erecv_sem.at[i], ((r + 1) % R, c)).wait_recv()
+        h, k = i // half, (y + 1 + i) % half
+        at = pl.ds(h * half, half)
+        return remote(esend.at[at], erecv.at[y, at], esend_sem.at[i], erecv_sem.at[y * per + h], (half + k, c))
+
+    def e_wait(i, h):
+        at = pl.ds(h * half, half)
+        remote(
+            esend.at[at], erecv.at[i, at], esend_sem.at[0], erecv_sem.at[i * per + h], ((r + 1) % R, c)
+        ).wait_recv()
 
     def x_copy(i):
         k, cc = i // C, i % C
-        return remote(esend.at[k], xrecv.at[y], xsend_sem.at[i], xrecv_sem.at[y], (t * share + k, cc))
+        return remote(
+            esend.at[k], xrecv.at[y, pl.ds(0, both)], xsend_sem.at[i], xrecv_sem.at[y], (t * share + k, cc)
+        )
 
     def x_wait(i):
-        remote(esend.at[0], xrecv.at[i], xsend_sem.at[0], xrecv_sem.at[i], ((r + 1) % R, c)).wait_recv()
+        remote(
+            esend.at[0], xrecv.at[i, pl.ds(0, both)], xsend_sem.at[0], xrecv_sem.at[i], ((r + 1) % R, c)
+        ).wait_recv()
 
     def f_copy(i):
-        return remote(fsend, frecv.at[y], fsend_sem.at[i], frecv_sem.at[y], (i // C, i % C))
+        at = pl.ds(both, nvec)
+        return remote(gsend.at[0, at], xrecv.at[y, at], fsend_sem.at[i], frecv_sem.at[y], (i // C, i % C))
 
     def f_wait(i):
-        remote(fsend, frecv.at[i], fsend_sem.at[0], frecv_sem.at[i], ((r + 1) % R, c)).wait_recv()
-
-    def both(i):
-        x_copy(i).start()
-        f_copy(i).start()
+        at = pl.ds(both, nvec)
+        remote(gsend.at[0, at], xrecv.at[i, at], fsend_sem.at[0], frecv_sem.at[i], ((r + 1) % R, c)).wait_recv()
+
+    def z_copy(i):
+        k, cc = i // C, i % C
+        return remote(gsend.at[k], xrecv.at[y], xsend_sem.at[i], xrecv_sem.at[y], (k, cc))
+
+    def z_wait(i):
+        remote(gsend.at[0], xrecv.at[i], xsend_sem.at[0], xrecv_sem.at[i], ((r + 1) % R, c)).wait_recv()
 
     def g_copy(i):
         return remote(gacc.at[i], grecv.at[i], gsend_sem.at[i], grecv_sem.at[i], (partner(i), c))
@@ -619,6 +632,11 @@
         for k in range(share):
             ref[k] = out[:, k * rows:(k + 1) * rows]
 
+    def put_pairs(ref, out):
+        for i in range(half):
+            for k in range(2):
+                ref[i, k] = out[:, (k * half + i) * rows:(k * half + i + 1) * rows]
+
     def inverse_times(hi, lo, values):
         left = jnp.concatenate([complex_left([v], nvec) for v in values], 1)
         return product(left, hi, lo, dot_nt)
@@ -637,35 +655,31 @@
         loads[0].wait()
         loads[1].wait()
         store(low_hi, low_lo, ..., pair(low_in))
-        put_slices(asend, inverse_times(low_hi[...], low_lo[...], [pair(kry_in, 0)]))
+        put_pairs(asend, inverse_times(low_hi[...], low_lo[...], [pair(kry_in, 0)]))
 
     arrive()
 
     @when(main & (t == 0))
     def _():
-        for d in range(1, share):
-            a_copy(d).start()
+        each(0, jnp.where(hub, half - 1, half), lambda i: a_copy(i).start())
 
     start_sends()
 
     @when(main & (t == 0))
     def _():
-        total = asend[p]
-        for d in range(1, share):
-            q = a_wait(d)
-            total = total + arecv[q]
-        ybuf[...] = total
-        pl.semaphore_wait(next_sem, 1)
-        for i in range(share - 1, -1, -1):
-            y_copy(i).start()
-
-        @when(z == 0)
-        def _():
-            y_hub().start()
-
-        each(0, half, lambda i: t_copy(i).start(), jnp.where(z == 1, y, half))
-
-        @when(z == 0)
+        @when(hub)
+        def _():
+            arecv[p] = asend[y]
+            each(0, share, a_wait, p)
+            parts = [arecv[q] for q in range(share)]
+            ybuf[...] = (parts[0] + parts[1]) + (parts[2] + parts[3])
+            pl.semaphore_wait(next_sem, 1)
+            for i in range(share):
+                y_copy(i).start()
+
+        each(0, half, lambda i: t_copy(i).start(), jnp.where(hub, y, half))
+
+        @when(jnp.logical_not(hub))
         def _():
             u_copy().start()
 
@@ -721,14 +735,11 @@
         def _():
             store(up_hi, up_lo, (slice(None), slice(0, span)), pair(up_in))
 
-        for q in range(share):
-            y_wait(q)
-        g = pair(kry_in, 0) - factor_times([yrecv[q] for q in range(share)], rows)
-        out = inverse_times(low_hi[...], low_lo[...], [g])
         for i in range(half):
-            for k in range(2):
-                dsend[i, k] = out[:, (k * half + i) * rows:(k * half + i + 1) * rows]
-        each(0, half, lambda i: d_copy(i).start(), jnp.where(hub, y, half))
+            y_wait(i)
+        g = pair(kry_in, 0) - factor_times([yrecv[q % half, q // half] for q in range(share)], rows)
+        put_pairs(dsend, inverse_times(low_hi[...], low_lo[...], [g]))
+        each(0, jnp.where(hub, half - 1, half), lambda i: d_copy(i).start())
         o_copy().start()
 
         @when(hub)
@@ -741,11 +752,11 @@
             parts = [drecv[q] for q in range(share)]
             total = (parts[0] + parts[1]) + (parts[2] + parts[3])
             put_slices(esend, inverse_times(up_hi[...], up_lo[...], [total[0], total[1]]))
-            for i in range(half):
+            for i in range(per * half):
                 e_copy(i).start()
             pl.semaphore_wait(all_sem, 1)
             each(0, share * C, lambda i: x_copy(i).start(), p * C + c)
-            xrecv[y] = esend[p]
+            xrecv[y, :both] = esend[p]
 
         end_from_side()
 
@@ -761,63 +772,76 @@
             )
             remote(upper, up_recv, usend_sem.at[0], urecv_sem.at[0], ((r + 1) % R, c)).wait_recv()
             store(up_hi, up_lo, (slice(None), slice(0, span)), pair(up_recv))
+            real, imag = [], []
             for k in range(2):
                 at = slice(k * span, (k + 1) * span)
                 out = product(stacked, up_hi[:, at], up_lo[:, at], dot_nn)
-                one = out[:nb, :rows] + out[nb:, rows:]
-                two = out[nb:, :rows] - out[:nb, rows:]
-                store(lead_hi, lead_lo, (slice(None), at), jnp.concatenate(
-                    [jnp.concatenate([one, two], 1), jnp.concatenate([-two, one], 1)], 0
-                ))
-            for k in range(2):
-                for h in range(per):
+                real.append(out[:nb, :rows] + out[nb:, rows:])
+                imag.append(out[:nb, rows:] - out[nb:, :rows])
+            real, imag = jnp.concatenate(real, 1), jnp.concatenate(imag, 1)
+            high, low = split(jnp.concatenate([real, imag], 1))
+            known = product(complex_left([ybuf[0], ybuf[1]], nvec), high, low, dot_nt)
+            for h in range(per):
+                for k in range(2):
                     m_wait(k, h)
                     store(
                         fac_hi, fac_lo, (slice(k * rows, (k + 1) * rows), slice(h * broad, (h + 1) * broad)),
                         pair(f_recv.at[k, h]),
                     )
-            y_wait(y)
-            yrecv[half + y] = ybuf[...]
             each(0, 2, o_wait)
-            for k in range(2):
-                one = gather_one[k]
-                high, low = split(jnp.concatenate([
-                    jnp.concatenate([one[0], one[1]], 1), jnp.concatenate([-one[1], one[0]], 1)
-                ], 0))
-                at = slice((2 + k) * span, (3 + k) * span)
-                lead_hi[:, at] = high
-                lead_lo[:, at] = low
+            empty = jnp.zeros((nb, rows), F32)
+            for h in range(per):
+                at = slice(h * broad, (h + 1) * broad)
+                out = product(
+                    jnp.concatenate([real, imag], 0), fac_hi[:span, at], fac_lo[:span, at], dot_nn
+                )
+                one = gather_one[h]
+                own_re = jnp.where(y == 0, jnp.concatenate([one[0], empty], 1), jnp.concatenate([empty, one[0]], 1))
+                own_im = jnp.where(y == 0, jnp.concatenate([one[1], empty], 1), jnp.concatenate([empty, one[1]], 1))
+                store(fac_hi, fac_lo, (slice(span, span + nb), at), jnp.concatenate([
+                    own_re - (out[:nb, :width] - out[nb:, width:]),
+                    -own_im - (out[:nb, width:] + out[nb:, :width]),
+                ], 1))
             pl.semaphore_wait(all_sem, 1)
 
-            for i in range(half):
-                e_wait(i)
-            x = [erecv[0, k] + erecv[1, k] for k in range(share)]
-            out = factor_times(x, 2 * rows)
-            w = [yrecv[k * half + y] - out[:, k * rows:(k + 1) * rows] for k in range(2)]
-            mine = [jnp.where(y == 0, x[k * half], x[k * half + 1]) for k in range(2)]
-            put_slices(esend, inverse_times(up_hi[...], up_lo[...], w))
-            fsend[...] = product(
-                jnp.concatenate([wide(v) for v in w + mine], 1), lead_hi[...], lead_lo[...], dot_nt
-            )
-            each(0, share * C, lambda i: both(i), p * C + c)
+            out = 0.0
+            for h in range(per):
+                for i in range(half):
+                    e_wait(i, h)
+                x = [erecv[0, h * half + k] + erecv[1, h * half + k] for k in range(half)]
+                at = slice(h * broad, (h + 1) * broad)
+                out = out + product(complex_left(x, nvec), fac_hi[:, at], fac_lo[:, at], dot_nt)
+            w = [ybuf[k] - out[:, k * rows:(k + 1) * rows] for k in range(2)]
+            first = wide(known + out[:, span:])
+            for k in range(share):
+                gsend[k, both:] = first
+            out = inverse_times(up_hi[...], up_lo[...], w)
+            for k in range(share):
+                gsend[k, :both] = out[:, k * rows:(k + 1) * rows]
+            each(0, share * C, lambda i: z_copy(i).start(), p * C + c)
             each(share * C, R * C, lambda i: f_copy(i).start())
-            xrecv[y] = esend[p]
-            frecv[y] = fsend[...]
+            xrecv[y] = gsend[p]
             end_from_side()
 
         @when(jnp.logical_not(hub))
         def _():
             end_from_side()
 
-    each(0, half, f_wait, jnp.where(hub & (t == 0), y, half))
-    first = frecv[0] + frecv[1]
-    ends = product(first, end_hi[...], end_lo[...], dot_nn)
+    @when(t == 0)
+    def _():
+        each(0, half, z_wait, jnp.where(hub, y, half))
+
+    @when(t == 1)
+    def _():
+        each(0, half, x_wait, jnp.where(hub, y, half))
+        each(0, half, f_wait)
+
+    total = xrecv[0] + xrecv[1]
+    ends = product(total[both:], end_hi[...], end_lo[...], dot_nn)
     coefficients[0] = ends[:, :nb]
     coefficients[1] = ends[:, nb:2 * nb]
-    each(0, half, x_wait, jnp.where(hub, y, half))
-    x = xrecv[0] + xrecv[1]
-    projected[0] = x[:nvec] - ends[:, 2 * nb:2 * nb + rows]
-    projected[1] = x[nvec:] - ends[:, 2 * nb + rows:]
+    projected[0] = total[:nvec] - ends[:, 2 * nb:2 * nb + rows]
+    projected[1] = total[nvec:both] - ends[:, 2 * nb + rows:]
 
     @when(side)
     def _():
@@ -841,33 +865,31 @@
 
         @when(t == 0)
         def _():
-            each(0, half, lambda i: t_copy(i).wait_send(), jnp.where(z == 1, y, half))
-            for d in range(1, share):
-                a_copy(d).wait_send()
-            for i in range(share):
-                y_copy(i).wait_send()
-
-            @when(z == 0)
+            each(0, half, lambda i: t_copy(i).wait_send(), jnp.where(hub, y, half))
+            each(0, jnp.where(hub, half - 1, half), lambda i: a_copy(i).wait_send())
+
+            @when(hub)
             def _():
-                y_hub().wait_send()
+                for i in range(share):
+                    y_copy(i).wait_send()
 
         @when(t == 1)
         def _():
             o_copy().wait_send()
-            each(0, half, lambda i: d_copy(i).wait_send(), jnp.where(hub, y, half))
+            each(0, jnp.where(hub, half - 1, half), lambda i: d_copy(i).wait_send())
 
         @when(hub)
         def _():
-            each(0, share * C, lambda i: x_copy(i).wait_send(), p * C + c)
-
             @when(t == 1)
             def _():
-                for i in range(half):
+                each(0, share * C, lambda i: x_copy(i).wait_send(), p * C + c)
+                for i in range(per * half):
                     e_copy(i).wait_send()
 
             @when(t == 0)
             def _():
-                each(0, R * C, lambda i: f_copy(i).wait_send(), me)
+                each(0, share * C, lambda i: z_copy(i).wait_send(), p * C + c)
+                each(share * C, R * C, lambda i: f_copy(i).wait_send())
 
 
 def hub_call(R, C, factor, lower, upper, krylov, basis):
@@ -890,15 +912,15 @@
         scratch_shapes=[
             f32(*factor.shape), f32(*lower.shape), f32(*upper.shape), f32(*krylov.shape), f32(*basis.shape),
             f32(*upper.shape), f32(2, per, *factor.shape),
-            *bf16(tile, 2 * rows), *bf16(tile, 4 * rows), *bf16(2 * rows, 2 * tile), *bf16(2 * nb, 8 * rows),
+            *bf16(tile, 2 * rows), *bf16(tile, 4 * rows), *bf16(2 * rows + nb, 2 * tile),
             *bf16(2 * nb, 2 * rows), *bf16(2 * nb, 2 * nb + 2 * rows),
             f32(share, *basis.shape), f32(2, *basis.shape),
-            f32(share, *block), f32(share, *block), f32(*block), f32(share, *block),
+            f32(half, 2, *block), f32(share, 2, *block), f32(2, *block), f32(half, 2, *block),
             f32(half, 2, *block), f32(share, 2, *block), f32(share, *block), f32(2, share, *block),
-            f32(half, *block), f32(nvec, 2 * nb), f32(half, nvec, 2 * nb),
+            f32(share, 3 * nvec, rows), f32(half, 3 * nvec, rows),
             f32(steps + 1, nb, 2 * nb), f32(steps + 1, nb, 2 * nb),
-            dma((5,)), dma((share,)), dma((share,)), dma((share + 1,)), dma((share,)),
-            dma((half,)), dma((share,)), dma((half,)), dma((half,)),
+            dma((5,)), dma((half,)), dma((share,)), dma((share,)), dma((half,)),
+            dma((half,)), dma((share,)), dma((per * half,)), dma((per * half,)),
             dma((share * C,)), dma((half,)), dma((R * C,)), dma((half,)),
             dma((1,)), dma((1,)), dma((1,)), dma((2 * per,)), dma((half,)), dma((share,)), dma((1,)), dma((2,)),
             dma((steps,)), dma((steps,)), dma((C,)), dma((1,)),

time: 23.4 us -> 23.4 us (level)
  no operation moved by 1% of the time
where the time goes in v3:
time: 23.4 us; the launch traced here: 23.3 us
  Pallas kernels  22.6 us (97%)
  between operations  0.64 us (3%)
    pallas_call x1, Pallas kernels, hub_call(): pl.pallas_call(functools.partial(hub_kernel, R, C), out_shape=(pltpu.VMEM...  22 us
    pallas_call x1, Pallas kernels, local(): pl.pallas_call(finish, out_shape=(jax.ShapeDtypeStruct(projected.shape, F...  0.63 us

profile of v3, /device:TPU:0, one launch (start us, length us, event | category | flops | bytes accessed | tf_op | source)
XLA Modules:
  0.0 23.3 jit_solution(17894194397035208135)
XLA Ops:
  0.6 22.0 %krylov_hubs.1 = (f32[2,16,128]{2,1,0:T(8,128)S(1)}, f32[2,16,64]{2,1,0:T(8,128)S(1)}) custom-call(f32[2,128,256]{2,1,0:T(8,128)} %factor.1, f32[2,512,128]{2,1,0:T(8,128)} %lower.1, f32[2,512,128]{2,1,0:T(8,128)} %upper.1, f32[2,16,128]{2,1,0:T(8,128)} %krylov.1, f32[2,64,128]{2,1,0:T(8,128)} %basis.1), custom_call_target="tpu_custom_call" | custom-call | tf_op jit(solution)/shard_map/krylov_hubs/pallas_call | solution.py:907
  22.6 0.6 %finish.1 = (f32[2,16,128]{2,1,0:T(8,128)}, f32[2,16,64]{2,1,0:T(8,128)}) custom-call(f32[2,16,128]{2,1,0:T(8,128)S(1)} %get-tuple-element.6.projected, f32[2,16,64]{2,1,0:T(8,128)S(1)} %get-tuple-element.7.turned), custom_call_target="tpu_custom_call" | custom-call | tf_op jit(solution)/shard_map/finish/pallas_call | solution.py:1017

commit v4 on v3

--- a/solution.py
+++ b/solution.py
@@ -390,14 +390,11 @@
 
 def hub_kernel(
     R, C, factor, lower, upper, krylov, basis, projected, coefficients,
-    fac_in, low_in, up_in, kry_in, bas_in, up_recv, f_recv,
+    fac_in, f_first, up_in, bas_in, up_recv, f_recv,
     low_hi, low_lo, up_hi, up_lo, fac_hi, fac_lo,
     bas_hi, bas_lo, end_hi, end_lo, gather, gather_one,
     asend, arecv, ybuf, yrecv, dsend, drecv, esend, erecv, gsend, xrecv, gacc, grecv,
-    load_sem, asend_sem, arecv_sem, ysend_sem, yrecv_sem, dsend_sem, drecv_sem,
-    esend_sem, erecv_sem, xsend_sem, xrecv_sem, fsend_sem, frecv_sem,
-    usend_sem, urecv_sem, msend_sem, mrecv_sem, tsend_sem, trecv_sem, osend_sem, orecv_sem,
-    gsend_sem, grecv_sem, hsend_sem, hrecv_sem, next_sem, all_sem,
+    load_sem, send_sem, recv_sem, next_sem, all_sem,
 ):
     tile, rows = lower.shape[1], lower.shape[2]
     width = factor.shape[2]
@@ -413,7 +410,6 @@
     t, p = r // share, r % share
     y, z = p % half, p // half
     lead = per - 1
-    both = 2 * nvec
     main = c == lead
     hub = main & (z == 1 - t)
     side = c == 0
@@ -426,24 +422,31 @@
             src_ref=src, dst_ref=dst, send_sem=send, recv_sem=recv, device_id=dest, device_id_type=MESH
         )
 
+    low_in, kry_in = f_first.at[:, pl.ds(0, tile)], f_first.at[:, pl.ds(tile, nvec)]
+
     def load(i, src, dst):
         return pltpu.make_async_copy(src, dst, load_sem.at[i])
 
-    loads = [
-        load(0, lower, low_in), load(1, krylov, kry_in), load(2, factor, fac_in), load(3, upper, up_in),
-        load(4, basis, bas_in),
-    ]
-
     @pl.when(main)
     def _():
-        for i in range(4):
-            loads[i].start()
-
-    loads[4].start()
+        load(0, lower, low_in).start()
+        load(0, krylov, kry_in).start()
+
+        @pl.when(t == 1)
+        def _():
+            load(1, factor, fac_in).start()
+
+        @pl.when(hub)
+        def _():
+            load(2, upper, up_in).start()
+
+    load(3, basis, bas_in).start()
 
     barrier = pltpu.get_barrier_semaphore()
     guide = (c == per) & (t == 1) & (z == 0)
     far = (c >= per) & (t == 0)
+    parted = far & (z == 0) & (c == per)
+    aid = (c == C - 1) & (t == 1) & (z == 1)
 
     def greet(rr, cc):
         pl.semaphore_signal(barrier, inc=1, device_id=(rr, cc), device_id_type=MESH)
@@ -465,8 +468,16 @@
         @pl.when(hub & (t == 0))
         def _():
             for cc in range(per, C):
+                greet(r, cc)
                 greet(y, cc)
-                greet(r, cc)
+
+        @pl.when(hub & (t == 1))
+        def _():
+            greet(share + half + y, C - 1)
+
+        @pl.when((t == 0) & (z == 0))
+        def _():
+            greet(r, per)
 
     @pl.when(side)
     def _():
@@ -485,9 +496,9 @@
     def arrive():
         count = jnp.where(main, jnp.where(hub, half - 1, half), jnp.where(
             side, steps + 1 + C - per + jnp.where((t == 0) & (z == 1), share, 0),
-            jnp.where(guide, R * C - 1, jnp.where(far, 1, 0)),
+            jnp.where(guide, R * C - 1, jnp.where(parted, 2, 1)),
         ))
-        @pl.when(main | side | far | guide)
+        @pl.when(main | side | far | guide | aid)
         def _():
             pl.semaphore_wait(barrier, count)
 
@@ -506,94 +517,75 @@
     def pair(ref, axis=1):
         return jnp.concatenate([ref[0], ref[1]], axis)
 
+    block, wave, bas, fac, ups, gram = 2 * nvec, 3 * nvec, 2 * nb, 2 * width, 2 * tile, 2 * nb * nb // rows
+    AD, US, MS, XS, YE, ES, TS, OS, GS = range(9)
+
+    def take(sem, count):
+        if count > ups:
+            ref = f_recv.at[:, :, :, pl.ds(0, count * rows // (4 * per * width))]
+        else:
+            ref = up_recv.at[:, pl.ds(0, count // 2)]
+        remote(ref, ref, send_sem.at[0], sem, ((r + 1) % R, c)).wait_recv()
+
+    def send(src, dst, recv, dest, way=0):
+        return remote(src, dst, send_sem.at[way], recv_sem.at[recv], dest)
+
     def a_copy(i):
         i = (y + 1 + i) % half
-        return remote(asend.at[i], arecv.at[p], asend_sem.at[i], arecv_sem.at[p], (half + i, c))
-
-    def a_wait(q):
-        remote(asend.at[0], arecv.at[q], asend_sem.at[0], arecv_sem.at[q], ((r + 1) % R, c)).wait_recv()
+        return send(asend.at[i], arecv.at[p], AD, (half + i, c))
 
     def y_copy(i):
         i = (1 - i // half) * half + (y + 1 + i) % half
-        return remote(ybuf, yrecv.at[y], ysend_sem.at[i], yrecv_sem.at[y], (share + i, c))
-
-    def y_wait(i):
-        remote(ybuf, yrecv.at[i], ysend_sem.at[0], yrecv_sem.at[i], ((r + 1) % R, c)).wait_recv()
-
-    def u_copy():
-        return remote(upper, up_recv, usend_sem.at[0], urecv_sem.at[0], (t * share + (1 - z) * half + y, c))
+        return send(ybuf, yrecv.at[y], YE, (share + i, c))
+
+    def u_copy(first, count):
+        at = pl.ds(first * (tile // 2), count * (tile // 2))
+        return send(upper.at[:, at], up_recv.at[:, at], US, (t * share + (1 - z) * half + y, lead))
 
     def m_near():
-        return remote(factor, f_recv.at[0, 0], msend_sem.at[0], mrecv_sem.at[0], (r, lead))
+        return send(factor, f_recv.at[0, 0], MS, (r, lead))
 
     def m_far():
-        h = c % per
-        return remote(factor, f_recv.at[z, h], msend_sem.at[0], mrecv_sem.at[z * per + h], (half + y, lead))
-
-    def m_wait(zz, h):
-        remote(factor, f_recv.at[zz, h], msend_sem.at[0], mrecv_sem.at[zz * per + h], ((r + 1) % R, c)).wait_recv()
+        return send(factor, f_recv.at[z, c % per], MS, (half + y, lead))
+
+    def m_part(i):
+        return send(factor.at[i], f_recv.at[0, 0, i], MS, (half * (1 - i) + y, lead))
+
+    def m_relay():
+        return send(f_recv.at[0, 0, 1], f_recv.at[0, 0, 1], MS, (half + y, lead))
 
     def t_copy(i):
-        return remote(basis, gather.at[p], tsend_sem.at[i], trecv_sem.at[p], (half + i, lead))
-
-    def t_wait(q):
-        remote(basis, gather.at[q], tsend_sem.at[0], trecv_sem.at[q], ((r + 1) % R, c)).wait_recv()
+        return send(basis, gather.at[p], TS, (half + i, lead))
 
     def o_copy():
-        return remote(basis, gather_one.at[z], osend_sem.at[0], orecv_sem.at[z], (half + y, lead))
-
-    def o_wait(zz):
-        remote(basis, gather_one.at[zz], osend_sem.at[0], orecv_sem.at[zz], ((r + 1) % R, c)).wait_recv()
+        return send(basis, gather_one.at[z], OS, (half + y, lead))
 
     def d_copy(i):
         i = (y + 1 + i) % half
-        return remote(dsend.at[i], drecv.at[p], dsend_sem.at[i], drecv_sem.at[p], (share + i, c))
-
-    def d_wait(q):
-        remote(dsend.at[0], drecv.at[q], dsend_sem.at[0], drecv_sem.at[q], ((r + 1) % R, c)).wait_recv()
+        return send(dsend.at[i], drecv.at[p], AD, (share + i, c))
 
     def e_copy(i):
         h, k = i // half, (y + 1 + i) % half
         at = pl.ds(h * half, half)
-        return remote(esend.at[at], erecv.at[y, at], esend_sem.at[i], erecv_sem.at[y * per + h], (half + k, c))
-
-    def e_wait(i, h):
-        at = pl.ds(h * half, half)
-        remote(
-            esend.at[at], erecv.at[i, at], esend_sem.at[0], erecv_sem.at[i * per + h], ((r + 1) % R, c)
-        ).wait_recv()
+        return send(esend.at[at], erecv.at[y, at], YE + h, (half + k, c))
 
     def x_copy(i):
         k, cc = i // C, i % C
-        return remote(
-            esend.at[k], xrecv.at[y, pl.ds(0, both)], xsend_sem.at[i], xrecv_sem.at[y], (t * share + k, cc)
-        )
-
-    def x_wait(i):
-        remote(
-            esend.at[0], xrecv.at[i, pl.ds(0, both)], xsend_sem.at[0], xrecv_sem.at[i], ((r + 1) % R, c)
-        ).wait_recv()
+        return send(esend.at[k], xrecv.at[y, pl.ds(0, block)], XS, (t * share + k, cc))
 
     def f_copy(i):
-        at = pl.ds(both, nvec)
-        return remote(gsend.at[0, at], xrecv.at[y, at], fsend_sem.at[i], frecv_sem.at[y], (i // C, i % C))
-
-    def f_wait(i):
-        at = pl.ds(both, nvec)
-        remote(gsend.at[0, at], xrecv.at[i, at], fsend_sem.at[0], frecv_sem.at[i], ((r + 1) % R, c)).wait_recv()
+        at = pl.ds(block, nvec)
+        return send(gsend.at[0, at], xrecv.at[y, at], XS, (i // C, i % C), 1)
 
     def z_copy(i):
         k, cc = i // C, i % C
-        return remote(gsend.at[k], xrecv.at[y], xsend_sem.at[i], xrecv_sem.at[y], (k, cc))
-
-    def z_wait(i):
-        remote(gsend.at[0], xrecv.at[i], xsend_sem.at[0], xrecv_sem.at[i], ((r + 1) % R, c)).wait_recv()
+        return send(gsend.at[k], xrecv.at[y], XS, (k, cc), 1)
 
     def g_copy(i):
-        return remote(gacc.at[i], grecv.at[i], gsend_sem.at[i], grecv_sem.at[i], (partner(i), c))
+        return send(gacc.at[i], grecv.at[i], GS + i, (partner(i), c))
 
     def h_copy(cc):
-        return remote(gacc.at[steps], grecv.at[steps], hsend_sem.at[cc], hrecv_sem.at[0], (r, cc))
+        return send(gacc.at[steps], grecv.at[steps], GS, (r, cc))
 
     def each(first_index, last_index, act, skip=None):
         def body(i, carry):
@@ -620,13 +612,22 @@
         def _():
             m_near().start()
 
-        @when(far)
+        @when(far & jnp.logical_not(parted))
         def _():
             m_far().start()
 
+        @when(parted)
+        def _():
+            for i in range(2):
+                m_part(1 - i).start()
+
         @when(main & (t == 1) & (z == 1))
         def _():
-            u_copy().start()
+            u_copy(0, 1).start()
+
+        @when(aid)
+        def _():
+            u_copy(1, 1).start()
 
     def put_slices(ref, out):
         for k in range(share):
@@ -647,13 +648,16 @@
         )
         return product(left, fac_hi[:count], fac_lo[:count], dot_nt)
 
+    def first_loads():
+        at = pl.ds(0, tile + nvec)
+        pltpu.make_async_copy(f_first.at[:, at], f_first.at[:, at], load_sem.at[0]).wait()
+
     span = 2 * rows
     broad = 2 * width
 
     @when(main & (t == 0))
     def _():
-        loads[0].wait()
-        loads[1].wait()
+        first_loads()
         store(low_hi, low_lo, ..., pair(low_in))
         put_pairs(asend, inverse_times(low_hi[...], low_lo[...], [pair(kry_in, 0)]))
 
@@ -670,7 +674,7 @@
         @when(hub)
         def _():
             arecv[p] = asend[y]
-            each(0, share, a_wait, p)
+            take(recv_sem.at[AD], (share - 1) * 2 * block)
             parts = [arecv[q] for q in range(share)]
             ybuf[...] = (parts[0] + parts[1]) + (parts[2] + parts[3])
             pl.semaphore_wait(next_sem, 1)
@@ -681,12 +685,11 @@
 
         @when(jnp.logical_not(hub))
         def _():
-            u_copy().start()
-
-        loads[2].wait()
-        loads[3].wait()
-
-    loads[4].wait()
+            u_copy(0, 2).start()
+            take(recv_sem.at[MS], fac // 2)
+            m_relay().start()
+
+    load(3, basis, bas_in).wait()
 
     def prepare_basis():
         top = pair(bas_in)
@@ -704,16 +707,15 @@
 
     def end_from_side():
         prepare_basis()
-        remote(gacc.at[0], grecv.at[steps], hsend_sem.at[0], hrecv_sem.at[0], (r, 0)).wait_recv()
+        take(recv_sem.at[GS], gram)
         prepare_end(grecv[steps])
 
     @when(side)
     def _():
         gacc[0] = product(prepare_basis(), bas_hi[...], bas_lo[...], dot_nt)
         for i in range(steps):
-            copy = g_copy(i)
-            copy.start()
-            copy.wait_recv()
+            g_copy(i).start()
+            take(recv_sem.at[GS + i], gram)
             gacc[i + 1] = gacc[i] + grecv[i]
         each(1, C, lambda cc: h_copy(cc).start())
         prepare_end(gacc[steps])
@@ -724,19 +726,19 @@
 
     @when(main & (t == 1))
     def _():
-        for i in range(4):
-            loads[i].wait()
+        first_loads()
+        load(1, factor, fac_in).wait()
         store(low_hi, low_lo, ..., pair(low_in))
         store(fac_hi, fac_lo, (slice(0, rows), slice(broad, 2 * broad)), pair(fac_in))
-        m_wait(0, 0)
+        take(recv_sem.at[MS], fac)
         store(fac_hi, fac_lo, (slice(0, rows), slice(0, broad)), pair(f_recv.at[0, 0]))
 
         @when(hub)
         def _():
+            load(2, upper, up_in).wait()
             store(up_hi, up_lo, (slice(None), slice(0, span)), pair(up_in))
 
-        for i in range(half):
-            y_wait(i)
+        take(recv_sem.at[YE], half * 2 * block)
         g = pair(kry_in, 0) - factor_times([yrecv[q % half, q // half] for q in range(share)], rows)
         put_pairs(dsend, inverse_times(low_hi[...], low_lo[...], [g]))
         each(0, jnp.where(hub, half - 1, half), lambda i: d_copy(i).start())
@@ -745,10 +747,10 @@
         @when(hub)
         def _():
             drecv[p] = dsend[y]
-            remote(upper, up_recv, usend_sem.at[0], urecv_sem.at[0], ((r + 1) % R, c)).wait_recv()
+            take(recv_sem.at[US], ups)
             store(up_hi, up_lo, (slice(None), slice(span, 2 * span)), pair(up_recv))
 
-            each(0, share, d_wait, p)
+            take(recv_sem.at[AD], (share - 1) * 2 * block)
             parts = [drecv[q] for q in range(share)]
             total = (parts[0] + parts[1]) + (parts[2] + parts[3])
             put_slices(esend, inverse_times(up_hi[...], up_lo[...], [total[0], total[1]]))
@@ -756,7 +758,7 @@
                 e_copy(i).start()
             pl.semaphore_wait(all_sem, 1)
             each(0, share * C, lambda i: x_copy(i).start(), p * C + c)
-            xrecv[y, :both] = esend[p]
+            xrecv[y, :block] = esend[p]
 
         end_from_side()
 
@@ -764,13 +766,14 @@
     def _():
         @when(hub)
         def _():
+            load(2, upper, up_in).wait()
             store(up_hi, up_lo, (slice(None), slice(span, 2 * span)), pair(up_in))
             gather[p] = bas_in[...]
-            each(0, share, t_wait, p)
+            take(recv_sem.at[TS], (share - 1) * bas)
             stacked = jnp.concatenate(
                 [jnp.concatenate([gather[q, i] for q in range(share)], 1) for i in range(2)], 0
             )
-            remote(upper, up_recv, usend_sem.at[0], urecv_sem.at[0], ((r + 1) % R, c)).wait_recv()
+            take(recv_sem.at[US], ups)
             store(up_hi, up_lo, (slice(None), slice(0, span)), pair(up_recv))
             real, imag = [], []
             for k in range(2):
@@ -781,14 +784,14 @@
             real, imag = jnp.concatenate(real, 1), jnp.concatenate(imag, 1)
             high, low = split(jnp.concatenate([real, imag], 1))
             known = product(complex_left([ybuf[0], ybuf[1]], nvec), high, low, dot_nt)
+            take(recv_sem.at[MS], 2 * per * fac)
             for h in range(per):
                 for k in range(2):
-                    m_wait(k, h)
                     store(
                         fac_hi, fac_lo, (slice(k * rows, (k + 1) * rows), slice(h * broad, (h + 1) * broad)),
                         pair(f_recv.at[k, h]),
                     )
-            each(0, 2, o_wait)
+            take(recv_sem.at[OS], 2 * bas)
             empty = jnp.zeros((nb, rows), F32)
             for h in range(per):
                 at = slice(h * broad, (h + 1) * broad)
@@ -806,18 +809,17 @@
 
             out = 0.0
             for h in range(per):
-                for i in range(half):
-                    e_wait(i, h)
+                take(recv_sem.at[YE + h], half * half * block)
                 x = [erecv[0, h * half + k] + erecv[1, h * half + k] for k in range(half)]
                 at = slice(h * broad, (h + 1) * broad)
                 out = out + product(complex_left(x, nvec), fac_hi[:, at], fac_lo[:, at], dot_nt)
             w = [ybuf[k] - out[:, k * rows:(k + 1) * rows] for k in range(2)]
             first = wide(known + out[:, span:])
             for k in range(share):
-                gsend[k, both:] = first
+                gsend[k, block:] = first
             out = inverse_times(up_hi[...], up_lo[...], w)
             for k in range(share):
-                gsend[k, :both] = out[:, k * rows:(k + 1) * rows]
+                gsend[k, :block] = out[:, k * rows:(k + 1) * rows]
             each(0, share * C, lambda i: z_copy(i).start(), p * C + c)
             each(share * C, R * C, lambda i: f_copy(i).start())
             xrecv[y] = gsend[p]
@@ -827,69 +829,37 @@
         def _():
             end_from_side()
 
-    @when(t == 0)
-    def _():
-        each(0, half, z_wait, jnp.where(hub, y, half))
-
-    @when(t == 1)
-    def _():
-        each(0, half, x_wait, jnp.where(hub, y, half))
-        each(0, half, f_wait)
+    @when(jnp.logical_not(hub))
+    def _():
+        take(recv_sem.at[XS], 2 * wave)
+
+    for i in range(2):
+        @when(hub & (t == i))
+        def _():
+            take(recv_sem.at[XS], wave + i * nvec)
 
     total = xrecv[0] + xrecv[1]
-    ends = product(total[both:], end_hi[...], end_lo[...], dot_nn)
+    ends = product(total[block:], end_hi[...], end_lo[...], dot_nn)
     coefficients[0] = ends[:, :nb]
     coefficients[1] = ends[:, nb:2 * nb]
     projected[0] = total[:nvec] - ends[:, 2 * nb:2 * nb + rows]
-    projected[1] = total[nvec:both] - ends[:, 2 * nb + rows:]
-
-    @when(side)
-    def _():
-        for i in range(steps):
-            g_copy(i).wait_send()
-        each(1, C, lambda cc: h_copy(cc).wait_send())
-
-        @when(t == 1)
-        def _():
-            m_near().wait_send()
-
-    @when((c >= per) & (t == 0))
-    def _():
-        m_far().wait_send()
-
-    @when(main)
-    def _():
-        @when(jnp.logical_not(hub))
-        def _():
-            u_copy().wait_send()
-
-        @when(t == 0)
-        def _():
-            each(0, half, lambda i: t_copy(i).wait_send(), jnp.where(hub, y, half))
-            each(0, jnp.where(hub, half - 1, half), lambda i: a_copy(i).wait_send())
-
-            @when(hub)
-            def _():
-                for i in range(share):
-                    y_copy(i).wait_send()
-
-        @when(t == 1)
-        def _():
-            o_copy().wait_send()
-            each(0, jnp.where(hub, half - 1, half), lambda i: d_copy(i).wait_send())
-
-        @when(hub)
-        def _():
-            @when(t == 1)
-            def _():
-                each(0, share * C, lambda i: x_copy(i).wait_send(), p * C + c)
-                for i in range(per * half):
-                    e_copy(i).wait_send()
-
-            @when(t == 0)
-            def _():
-                each(0, share * C, lambda i: z_copy(i).wait_send(), p * C + c)
-                each(share * C, R * C, lambda i: f_copy(i).wait_send())
+    projected[1] = total[nvec:block] - ends[:, 2 * nb + rows:]
+
+    def sent(cond, count, way=0):
+        @when(cond)
+        def _():
+            take(send_sem.at[way], count)
+
+    others = share * C - 1
+    sent(main & (t == 0) & (z == 0), half * (2 * block + bas) + ups + fac // 2)
+    sent(hub & (t == 0), (half - 1) * (2 * block + bas) + share * 2 * block)
+    sent(hub & (t == 0), others * wave + share * C * nvec, 1)
+    sent(main & (t == 1) & (z == 1), half * 2 * block + bas + ups // 2)
+    sent(hub & (t == 1), (half - 1) * 2 * block + bas + half * share * block + others * block)
+    sent(side & (t == 0), (steps + C - 1) * gram)
+    sent(side & (t == 1), (steps + C - 1) * gram + fac)
+    sent(far, fac)
+    sent(aid, ups // 2)
 
 
 def hub_call(R, C, factor, lower, upper, krylov, basis):
@@ -910,7 +880,7 @@
         in_specs=[pl.BlockSpec(memory_space=pl.ANY)] * 5,
         out_specs=(vmem, vmem),
         scratch_shapes=[
-            f32(*factor.shape), f32(*lower.shape), f32(*upper.shape), f32(*krylov.shape), f32(*basis.shape),
+            f32(*factor.shape), f32(2, tile + nvec, rows), f32(*upper.shape), f32(*basis.shape),
             f32(*upper.shape), f32(2, per, *factor.shape),
             *bf16(tile, 2 * rows), *bf16(tile, 4 * rows), *bf16(2 * rows + nb, 2 * tile),
             *bf16(2 * nb, 2 * rows), *bf16(2 * nb, 2 * nb + 2 * rows),
@@ -919,11 +889,7 @@
             f32(half, 2, *block), f32(share, 2, *block), f32(share, *block), f32(2, share, *block),
             f32(share, 3 * nvec, rows), f32(half, 3 * nvec, rows),
             f32(steps + 1, nb, 2 * nb), f32(steps + 1, nb, 2 * nb),
-            dma((5,)), dma((half,)), dma((share,)), dma((share,)), dma((half,)),
-            dma((half,)), dma((share,)), dma((per * half,)), dma((per * half,)),
-            dma((share * C,)), dma((half,)), dma((R * C,)), dma((half,)),
-            dma((1,)), dma((1,)), dma((1,)), dma((2 * per,)), dma((half,)), dma((share,)), dma((1,)), dma((2,)),
-            dma((steps,)), dma((steps,)), dma((C,)), dma((1,)),
+            dma((4,)), dma((2,)), dma((8 + steps,)),
             pltpu.SemaphoreType.REGULAR, pltpu.SemaphoreType.REGULAR,
         ],
         compiler_params=pltpu.CompilerParams(collective_id=0, has_side_effects=True),

time: 23.4 us -> 21.3 us (0.910)
  Pallas kernels: 22.6 us -> 20.5 us
    pallas_call x1, Pallas kernels: 22 us -> 19.9 us  [hub_call(): pl.pallas_call(functools.partial(hub_kernel, R, C), out_shape=(pltpu.VMEM...]
where the time goes in v4:
time: 21.3 us; the launch traced here: 21.1 us
  Pallas kernels  20.5 us (96%)
  between operations  0.64 us (3%)
    pallas_call x1, Pallas kernels, hub_call(): pl.pallas_call(functools.partial(hub_kernel, R, C), out_shape=(pltpu.VMEM...  19.9 us
    pallas_call x1, Pallas kernels, local(): pl.pallas_call(finish, out_shape=(jax.ShapeDtypeStruct(projected.shape, F...  0.63 us

profile of v4, /device:TPU:0, one launch (start us, length us, event | category | flops | bytes accessed | tf_op | source)
XLA Modules:
  0.0 21.1 jit_solution(15610320538471218232)
XLA Ops:
  0.6 19.9 %krylov_hubs.1 = (f32[2,16,128]{2,1,0:T(8,128)S(1)}, f32[2,16,64]{2,1,0:T(8,128)S(1)}) custom-call(f32[2,128,256]{2,1,0:T(8,128)} %factor.1, f32[2,512,128]{2,1,0:T(8,128)} %lower.1, f32[2,512,128]{2,1,0:T(8,128)} %upper.1, f32[2,16,128]{2,1,0:T(8,128)} %krylov.1, f32[2,64,128]{2,1,0:T(8,128)} %basis.1), custom_call_target="tpu_custom_call" | custom-call | tf_op jit(solution)/shard_map/krylov_hubs/pallas_call | solution.py:877
  20.5 0.6 %finish.1 = (f32[2,16,128]{2,1,0:T(8,128)}, f32[2,16,64]{2,1,0:T(8,128)}) custom-call(f32[2,16,128]{2,1,0:T(8,128)S(1)} %get-tuple-element.6.projected, f32[2,16,64]{2,1,0:T(8,128)S(1)} %get-tuple-element.7.turned), custom_call_target="tpu_custom_call" | custom-call | tf_op jit(solution)/shard_map/finish/pallas_call | solution.py:983

commit v5 on v4

--- a/solution.py
+++ b/solution.py
@@ -518,7 +518,8 @@
         return jnp.concatenate([ref[0], ref[1]], axis)
 
     block, wave, bas, fac, ups, gram = 2 * nvec, 3 * nvec, 2 * nb, 2 * width, 2 * tile, 2 * nb * nb // rows
-    AD, US, MS, XS, YE, ES, TS, OS, GS = range(9)
+    AD, US, XS, YE, ES, TS, VS, OS, GS = range(9)
+    MS = GS + steps
 
     def take(sem, count):
         if count > ups:
@@ -546,7 +547,7 @@
         return send(factor, f_recv.at[0, 0], MS, (r, lead))
 
     def m_far():
-        return send(factor, f_recv.at[z, c % per], MS, (half + y, lead))
+        return send(factor, f_recv.at[z, c % per], MS + z * per + c % per, (half + y, lead))
 
     def m_part(i):
         return send(factor.at[i], f_recv.at[0, 0, i], MS, (half * (1 - i) + y, lead))
@@ -554,8 +555,13 @@
     def m_relay():
         return send(f_recv.at[0, 0, 1], f_recv.at[0, 0, 1], MS, (half + y, lead))
 
-    def t_copy(i):
-        return send(basis, gather.at[p], TS, (half + i, lead))
+    def t_copy():
+        return send(basis, gather.at[p], TS, (half + y, lead))
+
+    def v_copy(i):
+        if i == 0:
+            return send(basis, gather.at[p], VS, (half + (y + 1) % half, lead))
+        return send(gather.at[y], gather.at[y], VS, (half + (y + 1) % half, lead))
 
     def o_copy():
         return send(basis, gather_one.at[z], OS, (half + y, lead))
@@ -629,10 +635,6 @@
         def _():
             u_copy(1, 1).start()
 
-    def put_slices(ref, out):
-        for k in range(share):
-            ref[k] = out[:, k * rows:(k + 1) * rows]
-
     def put_pairs(ref, out):
         for i in range(half):
             for k in range(2):
@@ -681,10 +683,13 @@
             for i in range(share):
                 y_copy(i).start()
 
-        each(0, half, lambda i: t_copy(i).start(), jnp.where(hub, y, half))
+        @when(hub)
+        def _():
+            v_copy(0).start()
 
         @when(jnp.logical_not(hub))
         def _():
+            t_copy().start()
             u_copy(0, 2).start()
             take(recv_sem.at[MS], fac // 2)
             m_relay().start()
@@ -736,7 +741,7 @@
         @when(hub)
         def _():
             load(2, upper, up_in).wait()
-            store(up_hi, up_lo, (slice(None), slice(0, span)), pair(up_in))
+            store(up_hi, up_lo, (slice(0, tile), slice(0, span)), pair(up_in))
 
         take(recv_sem.at[YE], half * 2 * block)
         g = pair(kry_in, 0) - factor_times([yrecv[q % half, q // half] for q in range(share)], rows)
@@ -748,14 +753,17 @@
         def _():
             drecv[p] = dsend[y]
             take(recv_sem.at[US], ups)
-            store(up_hi, up_lo, (slice(None), slice(span, 2 * span)), pair(up_recv))
+            store(up_hi, up_lo, (slice(0, tile), slice(span, 2 * span)), pair(up_recv))
 
             take(recv_sem.at[AD], (share - 1) * 2 * block)
             parts = [drecv[q] for q in range(share)]
             total = (parts[0] + parts[1]) + (parts[2] + parts[3])
-            put_slices(esend, inverse_times(up_hi[...], up_lo[...], [total[0], total[1]]))
-            for i in range(per * half):
-                e_copy(i).start()
+            out = inverse_times(up_hi[:tile], up_lo[:tile], [total[0], total[1]])
+            for h in range(per):
+                for k in range(half):
+                    esend[h * half + k] = out[:, (h * half + k) * rows:(h * half + k + 1) * rows]
+                for k in range(half):
+                    e_copy(h * half + k).start()
             pl.semaphore_wait(all_sem, 1)
             each(0, share * C, lambda i: x_copy(i).start(), p * C + c)
             xrecv[y, :block] = esend[p]
@@ -767,46 +775,38 @@
         @when(hub)
         def _():
             load(2, upper, up_in).wait()
-            store(up_hi, up_lo, (slice(None), slice(span, 2 * span)), pair(up_in))
+            store(up_hi, up_lo, (slice(0, tile), slice(span, 2 * span)), pair(up_in))
             gather[p] = bas_in[...]
-            take(recv_sem.at[TS], (share - 1) * bas)
+            take(recv_sem.at[TS], bas)
+            v_copy(1).start()
+            take(recv_sem.at[VS], 2 * bas)
             stacked = jnp.concatenate(
                 [jnp.concatenate([gather[q, i] for q in range(share)], 1) for i in range(2)], 0
             )
             take(recv_sem.at[US], ups)
-            store(up_hi, up_lo, (slice(None), slice(0, span)), pair(up_recv))
-            real, imag = [], []
+            store(up_hi, up_lo, (slice(0, tile), slice(0, span)), pair(up_recv))
             for k in range(2):
                 at = slice(k * span, (k + 1) * span)
-                out = product(stacked, up_hi[:, at], up_lo[:, at], dot_nn)
-                real.append(out[:nb, :rows] + out[nb:, rows:])
-                imag.append(out[:nb, rows:] - out[nb:, :rows])
-            real, imag = jnp.concatenate(real, 1), jnp.concatenate(imag, 1)
-            high, low = split(jnp.concatenate([real, imag], 1))
-            known = product(complex_left([ybuf[0], ybuf[1]], nvec), high, low, dot_nt)
-            take(recv_sem.at[MS], 2 * per * fac)
+                out = product(stacked, up_hi[:tile, at], up_lo[:tile, at], dot_nn)
+                store(up_hi, up_lo, (slice(tile, tile + nb), at), jnp.concatenate(
+                    [out[:nb, :rows] + out[nb:, rows:], out[:nb, rows:] - out[nb:, :rows]], 1
+                ))
+            take(recv_sem.at[OS], 2 * bas)
+            empty = jnp.zeros((nb, rows), F32)
+            for h in range(per):
+                at = slice(h * broad, (h + 1) * broad)
+                one = gather_one[h]
+                own_re = jnp.where(y == 0, jnp.concatenate([one[0], empty], 1), jnp.concatenate([empty, one[0]], 1))
+                own_im = jnp.where(y == 0, jnp.concatenate([one[1], empty], 1), jnp.concatenate([empty, one[1]], 1))
+                store(fac_hi, fac_lo, (slice(span, span + nb), at), jnp.concatenate([own_re, -own_im], 1))
+            pl.semaphore_wait(all_sem, 1)
             for h in range(per):
                 for k in range(2):
+                    take(recv_sem.at[MS + k * per + h], fac)
                     store(
                         fac_hi, fac_lo, (slice(k * rows, (k + 1) * rows), slice(h * broad, (h + 1) * broad)),
                         pair(f_recv.at[k, h]),
                     )
-            take(recv_sem.at[OS], 2 * bas)
-            empty = jnp.zeros((nb, rows), F32)
-            for h in range(per):
-                at = slice(h * broad, (h + 1) * broad)
-                out = product(
-                    jnp.concatenate([real, imag], 0), fac_hi[:span, at], fac_lo[:span, at], dot_nn
-                )
-                one = gather_one[h]
-                own_re = jnp.where(y == 0, jnp.concatenate([one[0], empty], 1), jnp.concatenate([empty, one[0]], 1))
-                own_im = jnp.where(y == 0, jnp.concatenate([one[1], empty], 1), jnp.concatenate([empty, one[1]], 1))
-                store(fac_hi, fac_lo, (slice(span, span + nb), at), jnp.concatenate([
-                    own_re - (out[:nb, :width] - out[nb:, width:]),
-                    -own_im - (out[:nb, width:] + out[nb:, :width]),
-                ], 1))
-            pl.semaphore_wait(all_sem, 1)
-
             out = 0.0
             for h in range(per):
                 take(recv_sem.at[YE + h], half * half * block)
@@ -814,13 +814,14 @@
                 at = slice(h * broad, (h + 1) * broad)
                 out = out + product(complex_left(x, nvec), fac_hi[:, at], fac_lo[:, at], dot_nt)
             w = [ybuf[k] - out[:, k * rows:(k + 1) * rows] for k in range(2)]
-            first = wide(known + out[:, span:])
+            more = inverse_times(up_hi[...], up_lo[...], w)
+            first = wide(out[:, span:] + more[:, tile:])
             for k in range(share):
                 gsend[k, block:] = first
-            out = inverse_times(up_hi[...], up_lo[...], w)
-            for k in range(share):
-                gsend[k, :block] = out[:, k * rows:(k + 1) * rows]
-            each(0, share * C, lambda i: z_copy(i).start(), p * C + c)
+            for h in range(per):
+                for k in range(h * half, (h + 1) * half):
+                    gsend[k, :block] = more[:, k * rows:(k + 1) * rows]
+                each(h * half * C, (h + 1) * half * C, lambda i: z_copy(i).start(), p * C + c)
             each(share * C, R * C, lambda i: f_copy(i).start())
             xrecv[y] = gsend[p]
             end_from_side()
@@ -851,8 +852,8 @@
             take(send_sem.at[way], count)
 
     others = share * C - 1
-    sent(main & (t == 0) & (z == 0), half * (2 * block + bas) + ups + fac // 2)
-    sent(hub & (t == 0), (half - 1) * (2 * block + bas) + share * 2 * block)
+    sent(main & (t == 0) & (z == 0), half * 2 * block + bas + ups + fac // 2)
+    sent(hub & (t == 0), (half - 1) * 2 * block + 2 * bas + share * 2 * block)
     sent(hub & (t == 0), others * wave + share * C * nvec, 1)
     sent(main & (t == 1) & (z == 1), half * 2 * block + bas + ups // 2)
     sent(hub & (t == 1), (half - 1) * 2 * block + bas + half * share * block + others * block)
@@ -882,14 +883,14 @@
         scratch_shapes=[
             f32(*factor.shape), f32(2, tile + nvec, rows), f32(*upper.shape), f32(*basis.shape),
             f32(*upper.shape), f32(2, per, *factor.shape),
-            *bf16(tile, 2 * rows), *bf16(tile, 4 * rows), *bf16(2 * rows + nb, 2 * tile),
+            *bf16(tile, 2 * rows), *bf16(tile + nb, 4 * rows), *bf16(2 * rows + nb, 2 * tile),
             *bf16(2 * nb, 2 * rows), *bf16(2 * nb, 2 * nb + 2 * rows),
             f32(share, *basis.shape), f32(2, *basis.shape),
             f32(half, 2, *block), f32(share, 2, *block), f32(2, *block), f32(half, 2, *block),
             f32(half, 2, *block), f32(share, 2, *block), f32(share, *block), f32(2, share, *block),
             f32(share, 3 * nvec, rows), f32(half, 3 * nvec, rows),
             f32(steps + 1, nb, 2 * nb), f32(steps + 1, nb, 2 * nb),
-            dma((4,)), dma((2,)), dma((8 + steps,)),
+            dma((4,)), dma((2,)), dma((8 + steps + 2 * per,)),
             pltpu.SemaphoreType.REGULAR, pltpu.SemaphoreType.REGULAR,
         ],
         compiler_params=pltpu.CompilerParams(collective_id=0, has_side_effects=True),

time: 21.3 us -> 21.5 us (level)
  no operation moved by 1% of the time
where the time goes in v5:
time: 21.5 us; the launch traced here: 21.3 us
  Pallas kernels  20.7 us (96%)
  between operations  0.64 us (3%)
    pallas_call x1, Pallas kernels, hub_call(): pl.pallas_call(functools.partial(hub_kernel, R, C), out_shape=(pltpu.VMEM...  20.1 us
    pallas_call x1, Pallas kernels, local(): pl.pallas_call(finish, out_shape=(jax.ShapeDtypeStruct(projected.shape, F...  0.63 us

profile of v5, /device:TPU:0, one launch (start us, length us, event | category | flops | bytes accessed | tf_op | source)
XLA Modules:
  0.0 21.3 jit_solution(16581986071866906057)
XLA Ops:
  0.6 20.1 %krylov_hubs.1 = (f32[2,16,128]{2,1,0:T(8,128)S(1)}, f32[2,16,64]{2,1,0:T(8,128)S(1)}) custom-call(f32[2,128,256]{2,1,0:T(8,128)} %factor.1, f32[2,512,128]{2,1,0:T(8,128)} %lower.1, f32[2,512,128]{2,1,0:T(8,128)} %upper.1, f32[2,16,128]{2,1,0:T(8,128)} %krylov.1, f32[2,64,128]{2,1,0:T(8,128)} %basis.1), custom_call_target="tpu_custom_call" | custom-call | tf_op jit(solution)/shard_map/krylov_hubs/pallas_call | solution.py:878
  20.7 0.6 %finish.1 = (f32[2,16,128]{2,1,0:T(8,128)}, f32[2,16,64]{2,1,0:T(8,128)}) custom-call(f32[2,16,128]{2,1,0:T(8,128)S(1)} %get-tuple-element.6.projected, f32[2,16,64]{2,1,0:T(8,128)S(1)} %get-tuple-element.7.turned), custom_call_target="tpu_custom_call" | custom-call | tf_op jit(solution)/shard_map/finish/pallas_call | solution.py:984

commit v6 on v5

--- a/solution.py
+++ b/solution.py
@@ -391,7 +391,7 @@
 def hub_kernel(
     R, C, factor, lower, upper, krylov, basis, projected, coefficients,
     fac_in, f_first, up_in, bas_in, up_recv, f_recv,
-    low_hi, low_lo, up_hi, up_lo, fac_hi, fac_lo,
+    low_hi, low_lo, up_hi, up_lo, fac_hi, fac_lo, turn_hi, turn_lo,
     bas_hi, bas_lo, end_hi, end_lo, gather, gather_one,
     asend, arecv, ybuf, yrecv, dsend, drecv, esend, erecv, gsend, xrecv, gacc, grecv,
     load_sem, send_sem, recv_sem, next_sem, all_sem,
@@ -640,15 +640,19 @@
             for k in range(2):
                 ref[i, k] = out[:, (k * half + i) * rows:(k * half + i + 1) * rows]
 
-    def inverse_times(hi, lo, values):
-        left = jnp.concatenate([complex_left([v], nvec) for v in values], 1)
-        return product(left, hi, lo, dot_nt)
-
-    def factor_times(values, count):
-        left = jnp.concatenate(
-            [complex_left(values[h * half:(h + 1) * half], nvec) for h in range(per)], 1
-        )
-        return product(left, fac_hi[:count], fac_lo[:count], dot_nt)
+    def times(values, high, low):
+        left = jnp.concatenate([complex_left(v, nvec) for v in values], 1)
+        return product(left, high, low, dot_nn)
+
+    def turn(hi, lo, row, col, value):
+        high, low = split(value.T)
+        at = (slice(row, row + value.shape[1]), slice(col, col + value.shape[0]))
+        hi[at] = high
+        lo[at] = low
+
+    def turn_pair(hi, lo, row, col, ref):
+        for i in range(2):
+            turn(hi, lo, row + i * ref.shape[2], col, ref[i])
 
     def first_loads():
         at = pl.ds(0, tile + nvec)
@@ -661,7 +665,8 @@
     def _():
         first_loads()
         store(low_hi, low_lo, ..., pair(low_in))
-        put_pairs(asend, inverse_times(low_hi[...], low_lo[...], [pair(kry_in, 0)]))
+        left = complex_left([pair(kry_in, 0)], nvec)
+        put_pairs(asend, product(left, low_hi[...], low_lo[...], dot_nt))
 
     arrive()
 
@@ -733,19 +738,25 @@
     def _():
         first_loads()
         load(1, factor, fac_in).wait()
-        store(low_hi, low_lo, ..., pair(low_in))
-        store(fac_hi, fac_lo, (slice(0, rows), slice(broad, 2 * broad)), pair(fac_in))
+        turn_pair(turn_hi, turn_lo, 0, 0, low_in)
+        turn_pair(fac_hi, fac_lo, broad, 0, fac_in)
         take(recv_sem.at[MS], fac)
-        store(fac_hi, fac_lo, (slice(0, rows), slice(0, broad)), pair(f_recv.at[0, 0]))
+        turn_pair(fac_hi, fac_lo, 0, 0, f_recv.at[0, 0])
 
         @when(hub)
         def _():
             load(2, upper, up_in).wait()
-            store(up_hi, up_lo, (slice(0, tile), slice(0, span)), pair(up_in))
+            turn_pair(up_hi, up_lo, 0, 0, up_in)
 
         take(recv_sem.at[YE], half * 2 * block)
-        g = pair(kry_in, 0) - factor_times([yrecv[q % half, q // half] for q in range(share)], rows)
-        put_pairs(dsend, inverse_times(low_hi[...], low_lo[...], [g]))
+        parts = [[yrecv[i, h] for i in range(half)] for h in range(per)]
+        g = pair(kry_in, 0) - times(parts, fac_hi[:, :rows], fac_lo[:, :rows])
+        ybuf[0] = g
+
+        @when(main)
+        def _():
+            put_pairs(dsend, times([[ybuf[0]]], turn_hi[...], turn_lo[...]))
+
         each(0, jnp.where(hub, half - 1, half), lambda i: d_copy(i).start())
         o_copy().start()
 
@@ -753,12 +764,12 @@
         def _():
             drecv[p] = dsend[y]
             take(recv_sem.at[US], ups)
-            store(up_hi, up_lo, (slice(0, tile), slice(span, 2 * span)), pair(up_recv))
+            turn_pair(up_hi, up_lo, span, 0, up_recv)
 
             take(recv_sem.at[AD], (share - 1) * 2 * block)
             parts = [drecv[q] for q in range(share)]
             total = (parts[0] + parts[1]) + (parts[2] + parts[3])
-            out = inverse_times(up_hi[:tile], up_lo[:tile], [total[0], total[1]])
+            out = times([[total[0]], [total[1]]], up_hi[:, :tile], up_lo[:, :tile])
             for h in range(per):
                 for k in range(half):
                     esend[h * half + k] = out[:, (h * half + k) * rows:(h * half + k + 1) * rows]
@@ -775,7 +786,7 @@
         @when(hub)
         def _():
             load(2, upper, up_in).wait()
-            store(up_hi, up_lo, (slice(0, tile), slice(span, 2 * span)), pair(up_in))
+            turn_pair(up_hi, up_lo, span, 0, up_in)
             gather[p] = bas_in[...]
             take(recv_sem.at[TS], bas)
             v_copy(1).start()
@@ -784,44 +795,50 @@
                 [jnp.concatenate([gather[q, i] for q in range(share)], 1) for i in range(2)], 0
             )
             take(recv_sem.at[US], ups)
-            store(up_hi, up_lo, (slice(0, tile), slice(0, span)), pair(up_recv))
+            turn_pair(up_hi, up_lo, 0, 0, up_recv)
             for k in range(2):
                 at = slice(k * span, (k + 1) * span)
-                out = product(stacked, up_hi[:tile, at], up_lo[:tile, at], dot_nn)
-                store(up_hi, up_lo, (slice(tile, tile + nb), at), jnp.concatenate(
-                    [out[:nb, :rows] + out[nb:, rows:], out[:nb, rows:] - out[nb:, :rows]], 1
-                ))
+                out = product(stacked, up_hi[at, :tile], up_lo[at, :tile], dot_nt)
+                turn(up_hi, up_lo, k * span, tile, out[:nb, :rows] + out[nb:, rows:])
+                turn(up_hi, up_lo, k * span + rows, tile, out[:nb, rows:] - out[nb:, :rows])
             take(recv_sem.at[OS], 2 * bas)
             empty = jnp.zeros((nb, rows), F32)
             for h in range(per):
-                at = slice(h * broad, (h + 1) * broad)
                 one = gather_one[h]
-                own_re = jnp.where(y == 0, jnp.concatenate([one[0], empty], 1), jnp.concatenate([empty, one[0]], 1))
-                own_im = jnp.where(y == 0, jnp.concatenate([one[1], empty], 1), jnp.concatenate([empty, one[1]], 1))
-                store(fac_hi, fac_lo, (slice(span, span + nb), at), jnp.concatenate([own_re, -own_im], 1))
+                for i in range(2):
+                    own = (1 - 2 * i) * one[i]
+                    own = jnp.where(y == 0, jnp.concatenate([own, empty], 1), jnp.concatenate([empty, own], 1))
+                    turn(fac_hi, fac_lo, h * broad + i * width, span, own)
             pl.semaphore_wait(all_sem, 1)
             for h in range(per):
                 for k in range(2):
                     take(recv_sem.at[MS + k * per + h], fac)
-                    store(
-                        fac_hi, fac_lo, (slice(k * rows, (k + 1) * rows), slice(h * broad, (h + 1) * broad)),
-                        pair(f_recv.at[k, h]),
-                    )
+                    turn_pair(fac_hi, fac_lo, h * broad, k * rows, f_recv.at[k, h])
             out = 0.0
             for h in range(per):
                 take(recv_sem.at[YE + h], half * half * block)
                 x = [erecv[0, h * half + k] + erecv[1, h * half + k] for k in range(half)]
                 at = slice(h * broad, (h + 1) * broad)
-                out = out + product(complex_left(x, nvec), fac_hi[:, at], fac_lo[:, at], dot_nt)
-            w = [ybuf[k] - out[:, k * rows:(k + 1) * rows] for k in range(2)]
-            more = inverse_times(up_hi[...], up_lo[...], w)
-            first = wide(out[:, span:] + more[:, tile:])
-            for k in range(share):
-                gsend[k, block:] = first
-            for h in range(per):
-                for k in range(h * half, (h + 1) * half):
+                out = out + times([x], fac_hi[at], fac_lo[at])
+            for k in range(2):
+                yrecv[0, k] = ybuf[k] - out[:, k * rows:(k + 1) * rows]
+            gsend[0, :, :nb] = jnp.concatenate([out[:, span:], out[:nvec, span:]], 0)
+
+            @when(main)
+            def _():
+                more = times([[yrecv[0, 0]], [yrecv[0, 1]]], up_hi[...], up_lo[...])
+                first = wide(gsend[0, :block, :nb] + more[:, tile:])
+                for k in range(share):
+                    gsend[k, block:] = first
                     gsend[k, :block] = more[:, k * rows:(k + 1) * rows]
-                each(h * half * C, (h + 1) * half * C, lambda i: z_copy(i).start(), p * C + c)
+                    for cc in range(C):
+                        if k < half or cc != lead:
+                            z_copy(k * C + cc).start()
+                        else:
+                            @when(p != k)
+                            def _():
+                                z_copy(k * C + cc).start()
+
             each(share * C, R * C, lambda i: f_copy(i).start())
             xrecv[y] = gsend[p]
             end_from_side()
@@ -883,7 +900,7 @@
         scratch_shapes=[
             f32(*factor.shape), f32(2, tile + nvec, rows), f32(*upper.shape), f32(*basis.shape),
             f32(*upper.shape), f32(2, per, *factor.shape),
-            *bf16(tile, 2 * rows), *bf16(tile + nb, 4 * rows), *bf16(2 * rows + nb, 2 * tile),
+            *bf16(tile, 2 * rows), *bf16(4 * rows, tile + nb), *bf16(2 * tile, 2 * rows + nb), *bf16(2 * rows, tile),
             *bf16(2 * nb, 2 * rows), *bf16(2 * nb, 2 * nb + 2 * rows),
             f32(share, *basis.shape), f32(2, *basis.shape),
             f32(half, 2, *block), f32(share, 2, *block), f32(2, *block), f32(half, 2, *block),

time: 21.5 us -> 20.9 us (0.972)
  Pallas kernels: 20.7 us -> 20.1 us
    pallas_call x1, Pallas kernels: 20.1 us -> 19.5 us  [hub_call(): pl.pallas_call(functools.partial(hub_kernel, R, C), out_shape=(pltpu.VMEM...]
where the time goes in v6:
time: 20.9 us; the launch traced here: 20.7 us
  Pallas kernels  20.1 us (96%)
  between operations  0.64 us (3%)
    pallas_call x1, Pallas kernels, hub_call(): pl.pallas_call(functools.partial(hub_kernel, R, C), out_shape=(pltpu.VMEM...  19.5 us
    pallas_call x1, Pallas kernels, local(): pl.pallas_call(finish, out_shape=(jax.ShapeDtypeStruct(projected.shape, F...  0.63 us

profile of v6, /device:TPU:0, one launch (start us, length us, event | category | flops | bytes accessed | tf_op | source)
XLA Modules:
  0.0 20.7 jit_solution(4897038326725134652)
XLA Ops:
  0.6 19.5 %krylov_hubs.1 = (f32[2,16,128]{2,1,0:T(8,128)S(1)}, f32[2,16,64]{2,1,0:T(8,128)S(1)}) custom-call(f32[2,128,256]{2,1,0:T(8,128)} %factor.1, f32[2,512,128]{2,1,0:T(8,128)} %lower.1, f32[2,512,128]{2,1,0:T(8,128)} %upper.1, f32[2,16,128]{2,1,0:T(8,128)} %krylov.1, f32[2,64,128]{2,1,0:T(8,128)} %basis.1), custom_call_target="tpu_custom_call" | custom-call | tf_op jit(solution)/shard_map/krylov_hubs/pallas_call | solution.py:895
  20.1 0.6 %finish.1 = (f32[2,16,128]{2,1,0:T(8,128)}, f32[2,16,64]{2,1,0:T(8,128)}) custom-call(f32[2,16,128]{2,1,0:T(8,128)S(1)} %get-tuple-element.6.projected, f32[2,16,64]{2,1,0:T(8,128)S(1)} %get-tuple-element.7.turned), custom_call_target="tpu_custom_call" | custom-call | tf_op jit(solution)/shard_map/finish/pallas_call | solution.py:1001

commit v7 on v6

--- a/solution.py
+++ b/solution.py
@@ -427,21 +427,6 @@
     def load(i, src, dst):
         return pltpu.make_async_copy(src, dst, load_sem.at[i])
 
-    @pl.when(main)
-    def _():
-        load(0, lower, low_in).start()
-        load(0, krylov, kry_in).start()
-
-        @pl.when(t == 1)
-        def _():
-            load(1, factor, fac_in).start()
-
-        @pl.when(hub)
-        def _():
-            load(2, upper, up_in).start()
-
-    load(3, basis, bas_in).start()
-
     barrier = pltpu.get_barrier_semaphore()
     guide = (c == per) & (t == 1) & (z == 0)
     far = (c >= per) & (t == 0)
@@ -492,6 +477,21 @@
         @pl.when(jnp.logical_not(guide & (y == i)))
         def _():
             greet(share + i, per)
+
+    @pl.when(main)
+    def _():
+        load(0, lower, low_in).start()
+        load(0, krylov, kry_in).start()
+
+        @pl.when(t == 1)
+        def _():
+            load(1, factor, fac_in).start()
+
+        @pl.when(hub)
+        def _():
+            load(2, upper, up_in).start()
+
+    load(3, basis, bas_in).start()
 
     def arrive():
         count = jnp.where(main, jnp.where(hub, half - 1, half), jnp.where(
@@ -654,11 +654,17 @@
         for i in range(2):
             turn(hi, lo, row + i * ref.shape[2], col, ref[i])
 
+    def turn_parts(row, ref):
+        for i in range(2):
+            for h in range(2):
+                turn(up_hi, up_lo, row + i * rows, h * gap, ref[i, h * width:(h + 1) * width])
+
     def first_loads():
         at = pl.ds(0, tile + nvec)
         pltpu.make_async_copy(f_first.at[:, at], f_first.at[:, at], load_sem.at[0]).wait()
 
     span = 2 * rows
+    gap = width + rows
     broad = 2 * width
 
     @when(main & (t == 0))
@@ -786,7 +792,7 @@
         @when(hub)
         def _():
             load(2, upper, up_in).wait()
-            turn_pair(up_hi, up_lo, span, 0, up_in)
+            turn_parts(span, up_in)
             gather[p] = bas_in[...]
             take(recv_sem.at[TS], bas)
             v_copy(1).start()
@@ -795,12 +801,14 @@
                 [jnp.concatenate([gather[q, i] for q in range(share)], 1) for i in range(2)], 0
             )
             take(recv_sem.at[US], ups)
-            turn_pair(up_hi, up_lo, 0, 0, up_recv)
+            turn_parts(0, up_recv)
             for k in range(2):
                 at = slice(k * span, (k + 1) * span)
-                out = product(stacked, up_hi[at, :tile], up_lo[at, :tile], dot_nt)
-                turn(up_hi, up_lo, k * span, tile, out[:nb, :rows] + out[nb:, rows:])
-                turn(up_hi, up_lo, k * span + rows, tile, out[:nb, rows:] - out[nb:, :rows])
+                high = jnp.concatenate([up_hi[at, :width], up_hi[at, gap:]], 1)
+                low = jnp.concatenate([up_lo[at, :width], up_lo[at, gap:]], 1)
+                out = product(stacked, high, low, dot_nt)
+                turn(up_hi, up_lo, k * span, width, out[:nb, :rows] + out[nb:, rows:])
+                turn(up_hi, up_lo, k * span + rows, width, out[:nb, rows:] - out[nb:, :rows])
             take(recv_sem.at[OS], 2 * bas)
             empty = jnp.zeros((nb, rows), F32)
             for h in range(per):
@@ -826,11 +834,14 @@
 
             @when(main)
             def _():
-                more = times([[yrecv[0, 0]], [yrecv[0, 1]]], up_hi[...], up_lo[...])
-                first = wide(gsend[0, :block, :nb] + more[:, tile:])
+                w = [[yrecv[0, 0]], [yrecv[0, 1]]]
+                more = times(w, up_hi[:, :width + nb], up_lo[:, :width + nb])
+                first = wide(gsend[0, :block, :nb] + more[:, width:])
                 for k in range(share):
+                    if k == half:
+                        more = times(w, up_hi[:, gap:], up_lo[:, gap:])
                     gsend[k, block:] = first
-                    gsend[k, :block] = more[:, k * rows:(k + 1) * rows]
+                    gsend[k, :block] = more[:, (k % half) * rows:(k % half + 1) * rows]
                     for cc in range(C):
                         if k < half or cc != lead:
                             z_copy(k * C + cc).start()
@@ -900,7 +911,7 @@
         scratch_shapes=[
             f32(*factor.shape), f32(2, tile + nvec, rows), f32(*upper.shape), f32(*basis.shape),
             f32(*upper.shape), f32(2, per, *factor.shape),
-            *bf16(tile, 2 * rows), *bf16(4 * rows, tile + nb), *bf16(2 * tile, 2 * rows + nb), *bf16(2 * rows, tile),
+            *bf16(tile, 2 * rows), *bf16(4 * rows, tile + rows), *bf16(2 * tile, 2 * rows + nb), *bf16(2 * rows, tile),
             *bf16(2 * nb, 2 * rows), *bf16(2 * nb, 2 * nb + 2 * rows),
             f32(share, *basis.shape), f32(2, *basis.shape),
             f32(half, 2, *block), f32(share, 2, *block), f32(2, *block), f32(half, 2, *block),

time: 20.9 us -> 20.7 us (level)
  no operation moved by 1% of the time
where the time goes in v7:
time: 20.7 us; the launch traced here: 20.6 us
  Pallas kernels  20 us (97%)
  between operations  0.64 us (3%)
    pallas_call x1, Pallas kernels, hub_call(): pl.pallas_call(functools.partial(hub_kernel, R, C), out_shape=(pltpu.VMEM...  19.3 us
    pallas_call x1, Pallas kernels, local(): pl.pallas_call(finish, out_shape=(jax.ShapeDtypeStruct(projected.shape, F...  0.63 us

profile of v7, /device:TPU:0, one launch (start us, length us, event | category | flops | bytes accessed | tf_op | source)
XLA Modules:
  0.0 20.6 jit_solution(809342928872733871)
XLA Ops:
  0.6 19.3 %krylov_hubs.1 = (f32[2,16,128]{2,1,0:T(8,128)S(1)}, f32[2,16,64]{2,1,0:T(8,128)S(1)}) custom-call(f32[2,128,256]{2,1,0:T(8,128)} %factor.1, f32[2,512,128]{2,1,0:T(8,128)} %lower.1, f32[2,512,128]{2,1,0:T(8,128)} %upper.1, f32[2,16,128]{2,1,0:T(8,128)} %krylov.1, f32[2,64,128]{2,1,0:T(8,128)} %basis.1), custom_call_target="tpu_custom_call" | custom-call | tf_op jit(solution)/shard_map/krylov_hubs/pallas_call | solution.py:906
  20.0 0.6 %finish.1 = (f32[2,16,128]{2,1,0:T(8,128)}, f32[2,16,64]{2,1,0:T(8,128)}) custom-call(f32[2,16,128]{2,1,0:T(8,128)S(1)} %get-tuple-element.6.projected, f32[2,16,64]{2,1,0:T(8,128)S(1)} %get-tuple-element.7.turned), custom_call_target="tpu_custom_call" | custom-call | tf_op jit(solution)/shard_map/finish/pallas_call | solution.py:1012

commit v8 on v7

--- a/solution.py
+++ b/solution.py
@@ -519,7 +519,7 @@
 
     block, wave, bas, fac, ups, gram = 2 * nvec, 3 * nvec, 2 * nb, 2 * width, 2 * tile, 2 * nb * nb // rows
     AD, US, XS, YE, ES, TS, VS, OS, GS = range(9)
-    MS = GS + steps
+    MS = GS + 1
 
     def take(sem, count):
         if count > ups:
@@ -588,7 +588,7 @@
         return send(gsend.at[k], xrecv.at[y], XS, (k, cc), 1)
 
     def g_copy(i):
-        return send(gacc.at[i], grecv.at[i], GS + i, (partner(i), c))
+        return send(gacc.at[i], grecv.at[i], MS + i, (partner(i), c))
 
     def h_copy(cc):
         return send(gacc.at[steps], grecv.at[steps], GS, (r, cc))
@@ -731,7 +731,7 @@
         gacc[0] = product(prepare_basis(), bas_hi[...], bas_lo[...], dot_nt)
         for i in range(steps):
             g_copy(i).start()
-            take(recv_sem.at[GS + i], gram)
+            take(recv_sem.at[MS + i], gram)
             gacc[i + 1] = gacc[i] + grecv[i]
         each(1, C, lambda cc: h_copy(cc).start())
         prepare_end(gacc[steps])
@@ -842,7 +842,7 @@
                         more = times(w, up_hi[:, gap:], up_lo[:, gap:])
                     gsend[k, block:] = first
                     gsend[k, :block] = more[:, (k % half) * rows:(k % half + 1) * rows]
-                    for cc in range(C):
+                    for cc in (range(C) if k != 1 else range(C - 1, -1, -1)):
                         if k < half or cc != lead:
                             z_copy(k * C + cc).start()
                         else:
@@ -918,7 +918,7 @@
             f32(half, 2, *block), f32(share, 2, *block), f32(share, *block), f32(2, share, *block),
             f32(share, 3 * nvec, rows), f32(half, 3 * nvec, rows),
             f32(steps + 1, nb, 2 * nb), f32(steps + 1, nb, 2 * nb),
-            dma((4,)), dma((2,)), dma((8 + steps + 2 * per,)),
+            dma((4,)), dma((2,)), dma((9 + max(steps, 2 * per),)),
             pltpu.SemaphoreType.REGULAR, pltpu.SemaphoreType.REGULAR,
         ],
         compiler_params=pltpu.CompilerParams(collective_id=0, has_side_effects=True),

time: 20.7 us -> 20.7 us (level)
  no operation moved by 1% of the time
where the time goes in v8:
time: 20.7 us; the launch traced here: 20.6 us
  Pallas kernels  19.9 us (96%)
  between operations  0.64 us (3%)
    pallas_call x1, Pallas kernels, hub_call(): pl.pallas_call(functools.partial(hub_kernel, R, C), out_shape=(pltpu.VMEM...  19.3 us
    pallas_call x1, Pallas kernels, local(): pl.pallas_call(finish, out_shape=(jax.ShapeDtypeStruct(projected.shape, F...  0.63 us

profile of v8, /device:TPU:0, one launch (start us, length us, event | category | flops | bytes accessed | tf_op | source)
XLA Modules:
  0.0 20.6 jit_solution(4481596910743299525)
XLA Ops:
  0.6 19.3 %krylov_hubs.1 = (f32[2,16,128]{2,1,0:T(8,128)S(1)}, f32[2,16,64]{2,1,0:T(8,128)S(1)}) custom-call(f32[2,128,256]{2,1,0:T(8,128)} %factor.1, f32[2,512,128]{2,1,0:T(8,128)} %lower.1, f32[2,512,128]{2,1,0:T(8,128)} %upper.1, f32[2,16,128]{2,1,0:T(8,128)} %krylov.1, f32[2,64,128]{2,1,0:T(8,128)} %basis.1), custom_call_target="tpu_custom_call" | custom-call | tf_op jit(solution)/shard_map/krylov_hubs/pallas_call | solution.py:906
  19.9 0.6 %finish.1 = (f32[2,16,128]{2,1,0:T(8,128)}, f32[2,16,64]{2,1,0:T(8,128)}) custom-call(f32[2,16,128]{2,1,0:T(8,128)S(1)} %get-tuple-element.6.projected, f32[2,16,64]{2,1,0:T(8,128)S(1)} %get-tuple-element.7.turned), custom_call_target="tpu_custom_call" | custom-call | tf_op jit(solution)/shard_map/finish/pallas_call | solution.py:1012

commit v9 on v8

--- a/solution.py
+++ b/solution.py
@@ -761,9 +761,20 @@
 
         @when(main)
         def _():
-            put_pairs(dsend, times([[ybuf[0]]], turn_hi[...], turn_lo[...]))
-
-        each(0, jnp.where(hub, half - 1, half), lambda i: d_copy(i).start())
+            out = times([[ybuf[0]]], turn_hi[...], turn_lo[...])
+            cut = [out[:, k * rows:(k + 1) * rows] for k in range(share)]
+            for j in range(half):
+                for k in range(2):
+                    dsend[(y + 1 + j) % half, k] = jnp.where(
+                        y == 0, cut[k * half + (1 + j) % half], cut[k * half + j % half]
+                    )
+                if j < half - 1:
+                    d_copy(j).start()
+                else:
+                    @when(jnp.logical_not(hub))
+                    def _():
+                        d_copy(j).start()
+
         o_copy().start()
 
         @when(hub)

time: 20.7 us -> 20.7 us (level)
  no operation moved by 1% of the time
where the time goes in v9:
time: 20.7 us; the launch traced here: 20.6 us
  Pallas kernels  19.9 us (96%)
  between operations  0.64 us (3%)
    pallas_call x1, Pallas kernels, hub_call(): pl.pallas_call(functools.partial(hub_kernel, R, C), out_shape=(pltpu.VMEM...  19.3 us
    pallas_call x1, Pallas kernels, local(): pl.pallas_call(finish, out_shape=(jax.ShapeDtypeStruct(projected.shape, F...  0.63 us

profile of v9, /device:TPU:0, one launch (start us, length us, event | category | flops | bytes accessed | tf_op | source)
XLA Modules:
  0.0 20.6 jit_solution(14900610934962474958)
XLA Ops:
  0.6 19.3 %krylov_hubs.1 = (f32[2,16,128]{2,1,0:T(8,128)S(1)}, f32[2,16,64]{2,1,0:T(8,128)S(1)}) custom-call(f32[2,128,256]{2,1,0:T(8,128)} %factor.1, f32[2,512,128]{2,1,0:T(8,128)} %lower.1, f32[2,512,128]{2,1,0:T(8,128)} %upper.1, f32[2,16,128]{2,1,0:T(8,128)} %krylov.1, f32[2,64,128]{2,1,0:T(8,128)} %basis.1), custom_call_target="tpu_custom_call" | custom-call | tf_op jit(solution)/shard_map/krylov_hubs/pallas_call | solution.py:917
  19.9 0.6 %finish.1 = (f32[2,16,128]{2,1,0:T(8,128)}, f32[2,16,64]{2,1,0:T(8,128)}) custom-call(f32[2,16,128]{2,1,0:T(8,128)S(1)} %get-tuple-element.6.projected, f32[2,16,64]{2,1,0:T(8,128)S(1)} %get-tuple-element.7.turned), custom_call_target="tpu_custom_call" | custom-call | tf_op jit(solution)/shard_map/finish/pallas_call | solution.py:1023
